TPU v7x, 256 devices: a whole 4x4x8 slice. The times are simulated.
256 devices in a mesh: rays: 64 (over z_hi, y, x), planes: 4 (over z_lo, core).
Axes of the slice: x: 4, y: 4, z: 8 (z_hi: 4, z_lo: 2; z = z_hi * 2 + z_lo), core: 2. Of those that a mesh axis runs over, the one named last changes fastest.
Arguments:
- tile_density: bfloat16 [4, 256, 128, 128], P(None, 'rays', 'planes'), may hold values from -6 to 6
- long_maps: bfloat16 [64, 4, 512, 2, 512], P('rays'), may hold values from -1.796875 to 1.796875
- map_owner: int32 [4], replicated, may hold values from 0 to 63
- tile_lists: int32 [64, 4, 64], replicated, may hold values from 0 to 255, as said below
- block_slots: int32 [4, 4096], P(None, ('rays', 'planes')), may hold values from 0 to 63
- block_windows: int32 [4, 2, 4096], P(None, None, ('rays', 'planes')), may hold values from 0 to 384
- fine_cells: int32 [4, 2, 2097152], P(None, None, ('rays', 'planes')), may hold values from 0 to 126
- long_cells: int32 [4, 2, 2097152], P(None, None, ('rays', 'planes')), may hold values from 0 to 126
- fractions: float32 [4, 4, 2097152], P(None, None, ('rays', 'planes')), may hold values from 0 to 1
Outputs:
- deflection: float32 [4, 2, 2097152], P(None, None, ('rays', 'planes'))
- source_shift: float32 [2, 2097152], P(None, ('rays', 'planes'))
Inputs may be any that keep to these rules, and one draw needn't show every extreme that they name: `tile_lists`: tile t belongs to owner t // 4. In each list of one bundle and plane at most 2 entries name tiles of one owner, and some owner has exactly 2 entries in every such list; entries may repeat.
All inputs are finite; a program needn't handle non-finite values.
Results may differ from a plain program's by a relative error of at most 0.0064.
Values may be sent and summed in bfloat16 or wider, within the bound.
No kernel may reach another device: no remote copies, remote signals or barrier semaphores. Data moves between devices by JAX's collectives and lax.ppermute only.
A program may use at most 128 MiB of HBM per device.

v0:
```python
import jax
import jax.numpy as jnp
from jax import lax
from jax.sharding import PartitionSpec as P

RATIO = 16


def spread(x, axis, root):
    mine = lax.axis_index(axis) == root
    return lax.psum(jnp.where(mine, x, jnp.zeros_like(x)), axis)


def kernel_tables(side):
    indices = jnp.arange(side, dtype=jnp.int32)
    offset = (indices[:, None] - indices[None, :]).astype(jnp.float32)
    tap_offsets = jnp.arange(-6, 7, dtype=jnp.int32).astype(jnp.float32)
    tap_total = jnp.sum(jnp.exp(-tap_offsets * tap_offsets / 8.0))
    inside = jnp.abs(offset) <= 6.0
    weight = jnp.where(inside, jnp.exp(-offset * offset / 8.0), 0.0) / tap_total
    smooth_table = weight.astype(jnp.bfloat16)
    slope_table = (6.0 * offset * weight / 4.0).astype(jnp.bfloat16)
    return (smooth_table, slope_table)


def convolve(density, smooth_table, slope_table):
    side = density.shape[1]
    right_table = jnp.concatenate([smooth_table.T, slope_table.T], axis=1)
    partial_value = jnp.einsum(
        "lij,jk->lik", density, right_table, preferred_element_type=jnp.float32
    ).astype(jnp.bfloat16)
    along_rows = jnp.einsum(
        "ij,ljk->lik", slope_table, partial_value[:, :, :side], preferred_element_type=jnp.float32
    )
    along_cols = jnp.einsum(
        "ij,ljk->lik", smooth_table, partial_value[:, :, side:], preferred_element_type=jnp.float32
    )
    return jnp.concatenate([along_rows, along_cols], axis=2).astype(jnp.bfloat16)


def interpolate(lookup, cell_row, cell_col, frac_row, frac_col):
    side = lookup.shape[1]
    positions = jnp.arange(side, dtype=jnp.int32)
    row_weight = jnp.where(positions == cell_row[..., None], 1.0 - frac_row[..., None], 0.0)
    row_weight = row_weight + jnp.where(
        positions == cell_row[..., None] + 1, frac_row[..., None], 0.0
    )
    col_weight = jnp.where(positions == cell_col[..., None], 1.0 - frac_col[..., None], 0.0)
    col_weight = col_weight + jnp.where(
        positions == cell_col[..., None] + 1, frac_col[..., None], 0.0
    )
    row_values = jnp.einsum(
        "bns,bsk->bnk", row_weight.astype(jnp.bfloat16), lookup, preferred_element_type=jnp.float32
    )
    along_x = jnp.sum(row_values[..., :side] * col_weight, axis=-1)
    along_y = jnp.sum(row_values[..., side:] * col_weight, axis=-1)
    return (along_x, along_y)


def map_windows(map_full, starts, side):

    def one_window(row_start, col_start):
        window = lax.dynamic_slice(map_full, (row_start, jnp.int32(0), col_start), (side, 2, side))
        return window.reshape(side, 2 * side)

    return jax.vmap(one_window)(starts[0], starts[1])


def lens_shift(previous, target, template):
    shifts = jnp.zeros_like(template)
    for earlier_plane, deflect in enumerate(previous[:target]):
        shifts = shifts - (target - earlier_plane) / target * deflect
    return shifts


def plane_step(fine_lookup, long_lookup, fine_cell, long_cell, offsets, shifts):
    fine_x, fine_y = interpolate(
        fine_lookup, fine_cell[0], fine_cell[1], offsets[0] + shifts[0], offsets[1] + shifts[1]
    )
    long_x, long_y = interpolate(
        long_lookup,
        long_cell[0],
        long_cell[1],
        offsets[2] + shifts[0] / RATIO,
        offsets[3] + shifts[1] / RATIO,
    )
    return jnp.stack([fine_x + long_x, fine_y + long_y])


def fetch_strips(store_rows, plane_lists, my_row, ray_count, capacity):
    tile_dev = store_rows.shape[0]
    list_len = plane_lists.shape[1]
    owners = plane_lists // tile_dev
    local_index = plane_lists % tile_dev
    list_positions = jnp.arange(list_len, dtype=jnp.int32)
    earlier = list_positions[:, None] > list_positions[None, :]
    same_owner = owners[:, :, None] == owners[:, None, :]
    rank_in_owner = jnp.sum(jnp.logical_and(same_owner, earlier[None]), axis=2)
    slot_ids = jnp.arange(capacity, dtype=jnp.int32)
    chosen = jnp.logical_and(
        owners[:, :, None] == my_row, rank_in_owner[:, :, None] == slot_ids[None, None, :]
    )
    send_index = jnp.sum(jnp.where(chosen, local_index[:, :, None], 0), axis=1)
    outgoing = jnp.take(store_rows, send_index.reshape(-1), axis=0)
    outgoing = outgoing.reshape(ray_count, capacity, store_rows.shape[1], store_rows.shape[2])
    incoming = lax.all_to_all(outgoing, "rays", split_axis=0, concat_axis=0, tiled=True)
    mine_owner = lax.dynamic_index_in_dim(owners, my_row, 0, keepdims=False)
    mine_rank = lax.dynamic_index_in_dim(rank_in_owner, my_row, 0, keepdims=False)
    flat_incoming = incoming.reshape(ray_count * capacity, store_rows.shape[1], store_rows.shape[2])
    return jnp.take(flat_incoming, mine_owner * capacity + mine_rank, axis=0)


def per_device(
    tile_density,
    long_maps,
    map_owner,
    tile_lists,
    block_slots,
    block_windows,
    fine_cells,
    long_cells,
    fractions,
):
    ray_count = lax.axis_size("rays")
    my_row = lax.axis_index("rays")
    tile_side = tile_density.shape[3]
    list_len = tile_lists.shape[2]
    capacity = 2 * list_len // ray_count
    plane_count = tile_density.shape[0]
    rays_here = fine_cells.shape[2]
    blocks = block_slots.shape[1]
    block_width = rays_here // blocks
    smooth_table, slope_table = kernel_tables(tile_side)
    fine_blocks = fine_cells.reshape(plane_count, 2, blocks, block_width)
    long_blocks = long_cells.reshape(plane_count, 2, blocks, block_width)
    frac_blocks = fractions.reshape(plane_count, 4, blocks, block_width)
    deflection_list = []
    for plane_index in range(plane_count):
        strip_rows = fetch_strips(
            tile_density[plane_index], tile_lists[:, plane_index, :], my_row, ray_count, capacity
        )
        full_tiles = lax.all_gather(strip_rows, "planes", axis=1, tiled=True)
        fields = convolve(full_tiles, smooth_table, slope_table)
        map_full = spread(long_maps[0, plane_index], "rays", map_owner[plane_index])
        fine_lookup = jnp.take(fields, block_slots[plane_index], axis=0)
        long_lookup = map_windows(map_full, block_windows[plane_index], tile_side)
        shifts = lens_shift(deflection_list, plane_index, frac_blocks[plane_index][:2])
        deflection_list.append(
            plane_step(
                fine_lookup,
                long_lookup,
                fine_blocks[plane_index],
                long_blocks[plane_index],
                frac_blocks[plane_index],
                shifts,
            )
        )
    source = lens_shift(deflection_list, plane_count, frac_blocks[0][:2])
    deflection = jnp.stack(deflection_list).reshape(plane_count, 2, rays_here)
    return (deflection, source.reshape(2, rays_here))


def solution(mesh):
    return jax.shard_map(
        per_device,
        mesh=mesh,
        in_specs=(
            P(None, "rays", "planes", None),
            P("rays", None, None, None, None),
            P(),
            P(),
            P(None, ("rays", "planes")),
            P(None, None, ("rays", "planes")),
            P(None, None, ("rays", "planes")),
            P(None, None, ("rays", "planes")),
            P(None, None, ("rays", "planes")),
        ),
        out_specs=(P(None, None, ("rays", "planes")), P(None, ("rays", "planes"))),
        check_vma=False,
    )
```

profile of v0, /device:TPU:2, one launch (start us, length us, event | category | flops | bytes accessed | tf_op | source)
XLA Modules:
  0.0 1166.7 jit_solution(9197577291111829367)
XLA Ops:
  12.1 6.1 fusion.99
  19.5 7.4 convert_reduce_fusion
  29.7 14.6 %all-to-all-start = ((bf16[64,2,32,128]{3,2,1,0:T(8,128)(2,1)}), bf16[64,2,32,128]{3,2,1,0:T(8,128)(2,1)S(1)}, u32[]{:S(2)}, u32[]{:S(2)}) async-start(bf16[64,2,32,128]{3,2,1,0:T(8,128)(2,1)} %bitcast.5), calls=%async_computation | async-start | bytes 2097152 | tf_op jit(solution)/shard_map/all_to_all | solution.py:106
  44.5 32.5 %all-to-all-done = bf16[64,2,32,128]{3,2,1,0:T(8,128)(2,1)S(1)} async-done(((bf16[64,2,32,128]{3,2,1,0:T(8,128)(2,1)}), bf16[64,2,32,128]{3,2,1,0:T(8,128)(2,1)S(1)}, u32[]{:S(2)}, u32[]{:S(2)}) %all-to-all-start) | async-done | bytes 1048608 | tf_op jit(solution)/shard_map/all_to_all | solution.py:106
  80.6 9.0 all-to-all-start.1
  97.6 32.3 %all-to-all-done.1 = bf16[64,2,32,128]{3,2,1,0:T(8,128)(2,1)S(1)} async-done(((bf16[64,2,32,128]{3,2,1,0:T(8,128)(2,1)}), bf16[64,2,32,128]{3,2,1,0:T(8,128)(2,1)S(1)}, u32[]{:S(2)}, u32[]{:S(2)}) %all-to-all-start.1) | async-done | bytes 1048608 | tf_op jit(solution)/shard_map/all_to_all | solution.py:106
  130.0 6.4 all-to-all-start.2
  152.3 9.1 all-to-all-done.2
  161.3 9.7 all-to-all-start.3
  190.2 18.4 %all-to-all-done.3 = bf16[64,2,32,128]{3,2,1,0:T(8,128)(2,1)S(1)} async-done(((bf16[64,2,32,128]{3,2,1,0:T(8,128)(2,1)}), bf16[64,2,32,128]{3,2,1,0:T(8,128)(2,1)S(1)}, u32[]{:S(2)}, u32[]{:S(2)}) %all-to-all-start.3) | async-done | bytes 1048608 | tf_op jit(solution)/shard_map/all_to_all | solution.py:106
  210.2 651.4 %all-reduce.3.cloned.1.call-done = (bf16[512,2,512]{2,1,0:T(2,128)(2,1)}, bf16[512,2,512]{2,1,0:T(2,128)(2,1)}, bf16[512,2,512]{2,1,0:T(2,128)(2,1)}, bf16[512,2,512]{2,1,0:T(2,128)(2,1)}) async-done(((bf16[512,2,512]{2,1,0:T(2,128)(2,1)}, bf16[512,2,512]{2,1,0:T(2,128)(2,1)}, bf16[512,2,512]{2,1,0:T(2,128)(2,1)}, bf16[512,2,512]{2,1,0:T(2,128)(2,1)}), (bf16[512,2,512]{2,1,0:T(2,128)(2,1)}, ...) | async-done | bytes 4194320 | tf_op jit(solution)/shard_map/psum | solution.py:11
  861.9 48.4 %while.4 = (s32[]{:T(128)}, bf16[512,2,512]{2,1,0:T(2,128)(2,1)}, s32[16,3]{0,1:T(4,128)S(1)}, bf16[16,128,2,128]{1,3,2,0:T(8,128)(2,1)S(1)}, s32[]{:T(128)}) while((s32[]{:T(128)}, bf16[512,2,512]{2,1,0:T(2,128)(2,1)}, s32[16,3]{0,1:T(4,128)S(1)}, bf16[16,128,2,128]{1,3,2,0:T(8,128)(2,1)S(1)}, s32[]{:T(128)}) %tuple.193), condition=%wide.while_cond, body=%wide.while_body.sunk | while | flops 2 | bytes 393333 | solution.py:63
  910.5 49.6 %while.5 = (s32[]{:T(128)}, bf16[512,2,512]{2,1,0:T(2,128)(2,1)}, s32[16,3]{0,1:T(4,128)S(1)}, bf16[16,128,2,128]{1,3,2,0:T(8,128)(2,1)S(1)}, s32[]{:T(128)}) while((s32[]{:T(128)}, bf16[512,2,512]{2,1,0:T(2,128)(2,1)}, s32[16,3]{0,1:T(4,128)S(1)}, bf16[16,128,2,128]{1,3,2,0:T(8,128)(2,1)S(1)}, s32[]{:T(128)}) %tuple.196), condition=%wide.while_cond.1, body=%wide.while_body.1.sunk | while | flops 2 | bytes 393333 | solution.py:63
  960.4 49.5 %while.6 = (s32[]{:T(128)}, bf16[512,2,512]{2,1,0:T(2,128)(2,1)}, s32[16,3]{0,1:T(4,128)S(1)}, bf16[16,128,2,128]{1,3,2,0:T(8,128)(2,1)S(1)}, s32[]{:T(128)}) while((s32[]{:T(128)}, bf16[512,2,512]{2,1,0:T(2,128)(2,1)}, s32[16,3]{0,1:T(4,128)S(1)}, bf16[16,128,2,128]{1,3,2,0:T(8,128)(2,1)S(1)}, s32[]{:T(128)}) %tuple.199), condition=%wide.while_cond.2, body=%wide.while_body.2.sunk | while | flops 2 | bytes 393333 | solution.py:63
  1010.1 48.4 %while.7 = (s32[]{:T(128)}, bf16[512,2,512]{2,1,0:T(2,128)(2,1)}, s32[16,3]{0,1:T(4,128)S(1)}, bf16[16,128,2,128]{1,3,2,0:T(8,128)(2,1)S(1)}, s32[]{:T(128)}) while((s32[]{:T(128)}, bf16[512,2,512]{2,1,0:T(2,128)(2,1)}, s32[16,3]{0,1:T(4,128)S(1)}, bf16[16,128,2,128]{1,3,2,0:T(8,128)(2,1)S(1)}, s32[]{:T(128)}) %tuple.202), condition=%wide.while_cond.3, body=%wide.while_body.3.sunk | while | flops 2 | bytes 393333 | solution.py:63
  1071.7 2.8 convolution_convert_fusion.2
  1088.2 2.8 convolution_convert_fusion
  1097.9 3.1 gather_fusion.2
  1105.8 4.7 pad_maximum_fusion.1
  1110.6 3.1 gather_fusion.5
  1123.4 4.8 pad_maximum_fusion.2
  1128.2 3.1 gather_fusion.8
  1141.3 4.0 pad_maximum_fusion.3
  1145.3 3.1 gather_fusion.11
  (709 shorter events, 315.3 us)
Async XLA Ops:
  8.0 853.6 %all-reduce.3.cloned.1.call-start = ((), (), s32[]{:S(2)}) async-start(), calls=%async_computation.8 | async-start | bytes 8388608 | tf_op jit(solution)/shard_map/psum | solution.py:11
  26.9 62.7 %copy-start.35 = (s32[64,64]{1,0:T(8,128)}, s32[64,64]{1,0:T(8,128)S(1)}, u32[]{:S(2)}) copy-start(s32[64,64]{1,0:T(8,128)S(1)} %get-tuple-element.87) | copy-start | bytes 49156
  29.7 47.3 %all-to-all-start = ((bf16[64,2,32,128]{3,2,1,0:T(8,128)(2,1)}), bf16[64,2,32,128]{3,2,1,0:T(8,128)(2,1)S(1)}, u32[]{:S(2)}, u32[]{:S(2)}) async-start(bf16[64,2,32,128]{3,2,1,0:T(8,128)(2,1)} %bitcast.5), calls=%async_computation | async-start | bytes 2097152 | tf_op jit(solution)/shard_map/all_to_all | solution.py:106
  44.4 1019.1 %all-gather.5.cloned.1.call-start = ((), (), s32[]{:S(2)}) async-start(), calls=%async_computation.4 | async-start | bytes 2621440 | tf_op jit(solution)/shard_map/all_gather | solution.py:142
  80.6 49.4 %all-to-all-start.1 = ((bf16[64,2,32,128]{3,2,1,0:T(8,128)(2,1)}), bf16[64,2,32,128]{3,2,1,0:T(8,128)(2,1)S(1)}, u32[]{:S(2)}, u32[]{:S(2)}) async-start(bf16[64,2,32,128]{3,2,1,0:T(8,128)(2,1)} %bitcast.25), calls=%async_computation.1 | async-start | bytes 2097152 | tf_op jit(solution)/shard_map/all_to_all | solution.py:106
  93.2 46.5 %copy-start.82 = (s32[8192]{0:T(1024)S(1)}, s32[8192]{0:T(1024)}, u32[]{:S(2)}) copy-start(s32[8192]{0:T(1024)} %get-tuple-element.234) | copy-start | bytes 98308
  93.2 46.7 %copy-start.79 = (s32[8192]{0:T(1024)S(1)}, s32[8192]{0:T(1024)}, u32[]{:S(2)}) copy-start(s32[8192]{0:T(1024)} %get-tuple-element.74) | copy-start | bytes 98308
  93.2 46.8 %copy-start.77 = (s32[8192]{0:T(1024)S(1)}, s32[8192]{0:T(1024)}, u32[]{:S(2)}) copy-start(s32[8192]{0:T(1024)} %get-tuple-element.73) | copy-start | bytes 98308
  93.2 46.8 %copy-start.76 = (s32[8192]{0:T(1024)S(1)}, s32[8192]{0:T(1024)}, u32[]{:S(2)}) copy-start(s32[8192]{0:T(1024)} %get-tuple-element.72) | copy-start | bytes 98308
  93.3 46.8 %copy-start.75 = (s32[8192]{0:T(1024)S(1)}, s32[8192]{0:T(1024)}, u32[]{:S(2)}) copy-start(s32[8192]{0:T(1024)} %get-tuple-element.236) | copy-start | bytes 98308
  97.6 42.2 %copy-start.86 = (f32[8192]{0:T(1024)S(1)}, f32[8192]{0:T(1024)}, u32[]{:S(2)}) copy-start(f32[8192]{0:T(1024)} %get-tuple-element.67) | copy-start | bytes 98308
  97.6 42.2 %copy-start.81 = (s32[8192]{0:T(1024)S(1)}, s32[8192]{0:T(1024)}, u32[]{:S(2)}) copy-start(s32[8192]{0:T(1024)} %get-tuple-element.235) | copy-start | bytes 98308
  97.6 42.2 %copy-start.85 = (f32[8192]{0:T(1024)S(1)}, f32[8192]{0:T(1024)}, u32[]{:S(2)}) copy-start(f32[8192]{0:T(1024)} %get-tuple-element.66) | copy-start | bytes 98308
  97.6 42.3 %copy-start.80 = (s32[8192]{0:T(1024)S(1)}, s32[8192]{0:T(1024)}, u32[]{:S(2)}) copy-start(s32[8192]{0:T(1024)} %get-tuple-element.75) | copy-start | bytes 98308
  97.6 42.3 %copy-start.84 = (f32[8192]{0:T(1024)S(1)}, f32[8192]{0:T(1024)}, u32[]{:S(2)}) copy-start(f32[8192]{0:T(1024)} %get-tuple-element.65) | copy-start | bytes 98308
  97.6 42.3 %copy-start.83 = (f32[8192]{0:T(1024)S(1)}, f32[8192]{0:T(1024)}, u32[]{:S(2)}) copy-start(f32[8192]{0:T(1024)} %get-tuple-element.64) | copy-start | bytes 98308
  97.6 47.1 %copy-start.89 = (s32[4,2,16]{2,1,0:T(2,128)S(1)}, s32[4,2,16]{2,1,0:T(2,128)}, u32[]{:S(2)}) copy-start(s32[4,2,16]{2,1,0:T(2,128)} %param.20) | copy-start | bytes 1540
  130.0 31.4 %all-to-all-start.2 = ((bf16[64,2,32,128]{3,2,1,0:T(8,128)(2,1)}), bf16[64,2,32,128]{3,2,1,0:T(8,128)(2,1)S(1)}, u32[]{:S(2)}, u32[]{:S(2)}) async-start(bf16[64,2,32,128]{3,2,1,0:T(8,128)(2,1)} %bitcast.43), calls=%async_computation.2 | async-start | bytes 2097152 | tf_op jit(solution)/shard_map/all_to_all | solution.py:106
  136.4 935.4 %all-gather.7.cloned.1.call-start = ((), (), s32[]{:S(2)}) async-start(), calls=%async_computation.5 | async-start | bytes 2621440 | tf_op jit(solution)/shard_map/all_gather | solution.py:142
  161.3 47.3 %all-to-all-start.3 = ((bf16[64,2,32,128]{3,2,1,0:T(8,128)(2,1)}), bf16[64,2,32,128]{3,2,1,0:T(8,128)(2,1)S(1)}, u32[]{:S(2)}, u32[]{:S(2)}) async-start(bf16[64,2,32,128]{3,2,1,0:T(8,128)(2,1)} %bitcast.61), calls=%async_computation.3 | async-start | bytes 2097152 | tf_op jit(solution)/shard_map/all_to_all | solution.py:106
  171.0 908.9 %all-gather.9.cloned.1.call-start = ((), (), s32[]{:S(2)}) async-start(), calls=%async_computation.6 | async-start | bytes 2621440 | tf_op jit(solution)/shard_map/all_gather | solution.py:142
  173.5 914.7 %all-gather.11.cloned.1.call-start = ((), (), s32[]{:S(2)}) async-start(), calls=%async_computation.7 | async-start | bytes 2621440 | tf_op jit(solution)/shard_map/all_gather | solution.py:142
  960.1 49.8 %copy-start.4 = (bf16[16,128,2,128]{1,3,2,0:T(8,128)(2,1)}, bf16[16,128,2,128]{1,3,2,0:T(8,128)(2,1)S(1)}, u32[]{:S(2)}) copy-start(bf16[16,128,2,128]{1,3,2,0:T(8,128)(2,1)S(1)} %get-tuple-element.20) | copy-start | bytes 3145732
  1009.9 51.3 %copy-start.5 = (bf16[16,128,2,128]{1,3,2,0:T(8,128)(2,1)}, bf16[16,128,2,128]{1,3,2,0:T(8,128)(2,1)S(1)}, u32[]{:S(2)}) copy-start(bf16[16,128,2,128]{1,3,2,0:T(8,128)(2,1)S(1)} %get-tuple-element.28) | copy-start | bytes 3145732
  (80 other events, 1220.8 us)
Sparse Core Ops, SparseCore 0:
  18.4 843.2 all-reduce.2
Sparse Core Ops, SparseCore 1:
  78.7 50.6 all-gather.4
  138.7 53.4 all-gather.6
  193.9 39.2 all-gather.8
  235.0 34.8 all-gather.10
where the time goes:
time: 1180 us; the launch traced here: 1170 us
  waiting for transfers between devices  744 us (63%)
  local copies, waits for them, and re-layouts  234 us (20%)
  other arithmetic  77.9 us (7%)
  matrix products  48 us (4%)
  starting transfers between devices  40.5 us (3%)
  between operations  20.8 us (2%)
    psum x1, waiting for transfers between devices, spread(): return lax.psum(jnp.where(mine, x, jnp.zeros_like(x)), axis)  651 us
    gather x320, local copies, waits for them, and re-layouts  194 us
    all_to_all x4, waiting for transfers between devices, fetch_strips(): lax.all_to_all(outgoing, 'rays', split_axis=0, concat_axis=0, tiled=True)  92.4 us
    all_to_all x4, starting transfers between devices, fetch_strips(): lax.all_to_all(outgoing, 'rays', split_axis=0, concat_axis=0, tiled=True)  39.8 us
  transfers between devices with their start and end apart: 9, of which 5 were waited for; matrix products, arithmetic and copies ran while one was open for 24% of the time, Pallas kernels for 0%

commit v1 on v0

v1 whole, which is shorter than its diff:
```python
import jax
import jax.numpy as jnp
from jax import lax
from jax.experimental import pallas as pl
from jax.experimental.pallas import tpu as pltpu
from jax.sharding import PartitionSpec as P

RATIO = 16
BF = jnp.bfloat16
F32 = jnp.float32
SUB = 16
ZG = 4
TAPS = 6


def kernel_tables(side):
    indices = jnp.arange(side, dtype=jnp.int32)
    offset = (indices[:, None] - indices[None, :]).astype(F32)
    tap_offsets = jnp.arange(-TAPS, TAPS + 1, dtype=jnp.int32).astype(F32)
    tap_total = jnp.sum(jnp.exp(-tap_offsets * tap_offsets / 8.0))
    inside = jnp.abs(offset) <= TAPS
    weight = jnp.where(inside, jnp.exp(-offset * offset / 8.0), 0.0) / tap_total
    smooth_table = weight.astype(BF)
    slope_table = (6.0 * offset * weight / 4.0).astype(BF)
    return (smooth_table, slope_table)


def with_next(table):
    following = jnp.concatenate([table[1:], jnp.zeros_like(table[:1])], axis=0)
    return jnp.concatenate([table.T, following.T], axis=1)


def onehot_tiles(row, tiles, width):
    wide = jnp.broadcast_to(row, (SUB, width)).astype(BF)
    place = lax.broadcasted_iota(jnp.int32, (SUB, width), 0).astype(F32)
    one = jnp.ones((SUB, width), BF)
    zero = jnp.zeros((SUB, width), BF)
    return [
        jnp.where(wide == (place + float(SUB * t)).astype(BF), one, zero) for t in range(tiles)
    ]


def corner_sums(parts, columns, select):
    rows, width = parts[0].shape
    tiles = rows // SUB
    here = onehot_tiles(columns, tiles, width)
    after = onehot_tiles(columns + 1.0, tiles, width)
    sums = []
    for part in parts:
        low = part.astype(BF)
        for hot in (here, after):
            total = low[:SUB] * hot[0]
            for t in range(1, tiles):
                total = total + low[t * SUB : (t + 1) * SUB] * hot[t]
            sums.append(total)
    stacked = jnp.concatenate(sums, axis=0)
    return jnp.dot(select, stacked, preferred_element_type=F32)[:8]


def fine_kernel(slot_ref, entry_ref, tiles_ref, cells_ref, left_ref, slope_ref, smooth_ref, select_ref, out_ref):
    step = pl.program_id(0)
    width = 512
    per_step = out_ref.shape[2] // width
    side = tiles_ref.shape[2]
    for b in range(per_step):
        slot = entry_ref[slot_ref[step * per_step + b]]
        density = tiles_ref[slot]
        lanes = slice(b * width, (b + 1) * width)
        partial = lax.dot_general(
            left_ref[...], density, (((1,), (1,)), ((), ())), preferred_element_type=F32
        ).astype(BF)
        along_x = jnp.dot(partial[:side], slope_ref[...], preferred_element_type=F32).astype(BF)
        along_y = jnp.dot(partial[side:], smooth_ref[...], preferred_element_type=F32).astype(BF)
        table = jnp.concatenate(
            [along_x[:, :side], along_y[:, :side], along_x[:, side:], along_y[:, side:]], axis=0
        )
        hot = jnp.concatenate(onehot_tiles(cells_ref[0, 0:1, lanes], side // SUB, width), axis=0)
        found = jnp.dot(table, hot, preferred_element_type=F32)
        parts = [found[i * side : (i + 1) * side] for i in range(4)]
        corners = corner_sums(parts, cells_ref[0, 1:2, lanes], select_ref[...])
        out_ref[0, :, lanes] = corners.astype(BF)


def long_kernel(start_ref, map_ref, next_ref, cells_ref, select_ref, out_ref):
    step = pl.program_id(0)
    width = 512
    per_step = out_ref.shape[2] // width
    extent = map_ref.shape[1]
    side = 128
    rows = side + SUB
    for b in range(per_step):
        block = step * per_step + b
        row_start = start_ref[0, block]
        col_start = start_ref[1, block]
        row_base = jnp.minimum(row_start // side, extent // side - 2) * side
        col_base = jnp.minimum(col_start // SUB, (extent - rows) // SUB) * SUB
        row_base = pl.multiple_of(row_base, side)
        col_base = pl.multiple_of(col_base, SUB)
        lanes = slice(b * width, (b + 1) * width)
        take = (pl.ds(col_base, rows), pl.ds(row_base, 2 * side))
        table = jnp.concatenate(
            [map_ref[(0, *take)], map_ref[(1, *take)], next_ref[(0, *take)], next_ref[(1, *take)]],
            axis=0,
        )
        row = cells_ref[0, 2:3, lanes] + (row_start - row_base).astype(F32)
        col = cells_ref[0, 3:4, lanes] + (col_start - col_base).astype(F32)
        hot = jnp.concatenate(onehot_tiles(row, 2 * side // SUB, width), axis=0)
        found = jnp.dot(table, hot, preferred_element_type=F32)
        parts = [found[i * rows : (i + 1) * rows] for i in range(4)]
        out_ref[0, :, lanes] = corner_sums(parts, col, select_ref[...]).astype(BF)


def table_value(corners, p, q):
    rw0 = (1.0 - p).astype(BF).astype(F32)
    rw1 = p.astype(BF).astype(F32)
    cw0, cw1 = 1.0 - q, q
    v = [corners[i : i + 1] for i in range(8)]
    along_x = (rw0 * v[0] + rw1 * v[4]) * cw0 + (rw0 * v[1] + rw1 * v[5]) * cw1
    along_y = (rw0 * v[2] + rw1 * v[6]) * cw0 + (rw0 * v[3] + rw1 * v[7]) * cw1
    return along_x, along_y


def lens_shift(previous, target):
    shift_x, shift_y = 0.0, 0.0
    for earlier, (x, y) in enumerate(previous):
        factor = (target - earlier) / target
        shift_x, shift_y = shift_x - factor * x, shift_y - factor * y
    return shift_x, shift_y


def final_kernel(fine_ref, long_ref, frac_ref, deflection_ref, source_ref):
    planes = fine_ref.shape[0]
    found = []
    for k in range(planes):
        frac = frac_ref[k]
        sx, sy = lens_shift(found, k)
        fx, fy = table_value(fine_ref[k].astype(F32), frac[0:1] + sx, frac[1:2] + sy)
        lx, ly = table_value(
            long_ref[k].astype(F32), frac[2:3] + sx / RATIO, frac[3:4] + sy / RATIO
        )
        found.append((fx + lx, fy + ly))
        deflection_ref[k, 0:1] = found[k][0]
        deflection_ref[k, 1:2] = found[k][1]
    sx, sy = lens_shift(found, planes)
    source_ref[0:1] = sx
    source_ref[1:2] = sy


def per_device(
    tile_density,
    long_maps,
    map_owner,
    tile_lists,
    block_slots,
    block_windows,
    fine_cells,
    long_cells,
    fractions,
):
    my_row = lax.axis_index("rays")
    plane = lax.axis_index("planes")
    planes, tile_dev, strip, side = tile_density.shape
    extent = long_maps.shape[2]
    list_len = tile_lists.shape[2]
    rays_here = fine_cells.shape[2]
    blocks = block_slots.shape[1]
    ray_count = lax.axis_size("rays")
    level = ray_count // ZG
    my_z, my_xy = my_row // level, my_row % level
    flat_groups = [[z * level + i for i in range(level)] for z in range(ZG)]

    def along_z(x, d):
        pairs = [(r, (r // level + d) % ZG * level + r % level) for r in range(ray_count)]
        return lax.ppermute(x, "rays", pairs)

    def exchange_flat(x):
        return lax.all_to_all(x, "rays", 0, 0, tiled=True, axis_index_groups=flat_groups)

    small = jnp.concatenate(
        [
            block_slots[:, None, :],
            block_windows // SUB,
            block_windows % SUB,
        ],
        axis=1,
    ).reshape(planes, 1, 5 * blocks)
    small = jnp.pad(small, ((0, 0), (0, 3), (0, 128 - 5 * blocks)))
    cells = jnp.concatenate([fine_cells, long_cells], axis=1)
    ray_info = jnp.concatenate([cells, small], axis=2).astype(BF)
    ray_info = lax.all_to_all(ray_info, "planes", 0, 0, tiled=True)
    cells = ray_info[:, :, :rays_here].astype(F32)
    small = ray_info[:, 0, rays_here : rays_here + 5 * blocks].astype(jnp.int32)
    small = small.reshape(planes, 5, blocks)
    slots = small[:, 0].reshape(planes * blocks)
    starts = (small[:, 1:3] * SUB + small[:, 3:5]).transpose(1, 0, 2).reshape(2, planes * blocks)

    tiles = lax.all_to_all(tile_density, "planes", 0, 0, tiled=True)
    tiles = tiles.transpose(1, 0, 2, 3).reshape(tile_dev, side, side)
    column = jnp.stack([tiles] + [along_z(tiles, d) for d in range(1, ZG)])
    level_lists = lax.dynamic_slice(tile_lists, (my_z * level, plane, 0), (level, 1, list_len))[:, 0]
    owners = level_lists // tile_dev
    key = jnp.arange(list_len, dtype=jnp.int32) * tile_dev + level_lists % tile_dev
    column_owner = (my_z - jnp.arange(ZG, dtype=jnp.int32)) % ZG * level + my_xy
    mine = owners[:, None, :] == column_owner[None, :, None]
    first = jnp.min(jnp.where(mine, key[:, None, :], tile_dev * list_len), axis=2) % tile_dev
    last = jnp.max(jnp.where(mine, key[:, None, :], 0), axis=2) % tile_dev
    wanted = jnp.stack([first, last], axis=2)[:, :, :, None, None]
    outgoing = jnp.broadcast_to(column[None, :, None, 0], (level, ZG, 2, side, side))
    for t in range(1, tile_dev):
        outgoing = jnp.where(wanted == t, column[None, :, None, t], outgoing)
    incoming = exchange_flat(outgoing).reshape(level * ZG * 2, side, side)

    my_list = lax.dynamic_slice(tile_lists, (my_row, plane, 0), (1, 1, list_len))[0, 0]
    my_owner = my_list // tile_dev
    place = jnp.arange(list_len, dtype=jnp.int32)
    repeat = (my_owner[:, None] == my_owner[None, :]) & (place[:, None] > place[None, :])
    rank = jnp.max(repeat.astype(jnp.int32), axis=1)
    entry = my_owner % level * (2 * ZG) + (my_z - my_owner // level) % ZG * 2 + rank

    own_map = lax.dynamic_index_in_dim(long_maps[0], plane, 0, keepdims=False)
    own_map = own_map.transpose(1, 2, 0).reshape(level, 2 * extent // level, extent)
    owner = lax.dynamic_index_in_dim(map_owner, plane, 0, keepdims=False)
    pieces = exchange_flat(own_map)
    piece = lax.dynamic_index_in_dim(pieces, owner % level, 0, keepdims=False)
    distance = (my_z - owner // level) % ZG
    chosen = piece
    for d in range(1, ZG):
        chosen = jnp.where(distance == d, along_z(piece, d), chosen)
    whole = exchange_flat(jnp.broadcast_to(chosen[None], (level, *chosen.shape)))
    whole = whole.reshape(2, extent, extent)
    following = jnp.concatenate([whole[:, :, 1:], whole[:, :, :1]], axis=2)

    select = (jnp.arange(8 * SUB)[None, :] // SUB == jnp.arange(SUB)[:, None]).astype(BF)
    smooth_table, slope_table = kernel_tables(side)
    left = jnp.concatenate([smooth_table, slope_table], axis=0)
    wide = 2048
    per_plane = rays_here // wide
    vmem = pl.BlockSpec(memory_space=pltpu.VMEM)
    cell_spec = pl.BlockSpec((1, 4, wide), lambda g, *_: (g // per_plane, 0, g % per_plane))
    out_spec = pl.BlockSpec((1, 8, wide), lambda g, *_: (g // per_plane, 0, g % per_plane))
    corner_shape = jax.ShapeDtypeStruct((planes, 8, rays_here), BF)
    params = pltpu.CompilerParams(vmem_limit_bytes=48 << 20)
    long_corners = pl.pallas_call(
        long_kernel,
        out_shape=corner_shape,
        grid_spec=pltpu.PrefetchScalarGridSpec(
            num_scalar_prefetch=1,
            grid=(planes * per_plane,),
            in_specs=[vmem, vmem, cell_spec, vmem],
            out_specs=out_spec,
        ),
        compiler_params=params,
        name="long_gather",
    )(starts, whole, following, cells, select)
    long_corners = lax.all_to_all(long_corners, "planes", 0, 0, tiled=True)
    fine_corners = pl.pallas_call(
        fine_kernel,
        out_shape=corner_shape,
        grid_spec=pltpu.PrefetchScalarGridSpec(
            num_scalar_prefetch=2,
            grid=(planes * per_plane,),
            in_specs=[vmem, cell_spec, vmem, vmem, vmem, vmem],
            out_specs=out_spec,
        ),
        compiler_params=params,
        name="fine_gather",
    )(slots, entry, incoming, cells, left, with_next(slope_table), with_next(smooth_table), select)
    fine_corners = lax.all_to_all(fine_corners, "planes", 0, 0, tiled=True)

    return pl.pallas_call(
        final_kernel,
        out_shape=(
            jax.ShapeDtypeStruct((planes, 2, rays_here), F32),
            jax.ShapeDtypeStruct((2, rays_here), F32),
        ),
        grid=(per_plane,),
        in_specs=[
            pl.BlockSpec((planes, 8, wide), lambda g: (0, 0, g)),
            pl.BlockSpec((planes, 8, wide), lambda g: (0, 0, g)),
            pl.BlockSpec((planes, 4, wide), lambda g: (0, 0, g)),
        ],
        out_specs=(
            pl.BlockSpec((planes, 2, wide), lambda g: (0, 0, g)),
            pl.BlockSpec((2, wide), lambda g: (0, g)),
        ),
        name="lens_sum",
    )(fine_corners, long_corners, fractions)


def solution(mesh):
    return jax.shard_map(
        per_device,
        mesh=mesh,
        in_specs=(
            P(None, "rays", "planes", None),
            P("rays", None, None, None, None),
            P(),
            P(),
            P(None, ("rays", "planes")),
            P(None, None, ("rays", "planes")),
            P(None, None, ("rays", "planes")),
            P(None, None, ("rays", "planes")),
            P(None, None, ("rays", "planes")),
        ),
        out_specs=(P(None, None, ("rays", "planes")), P(None, ("rays", "planes"))),
        check_vma=False,
    )
```

time: 1180 us -> 204 us (0.17)
  the two profiles are of different devices: /device:TPU:2 before, /device:TPU:1 now
where the time goes in v1:
time: 204 us; the launch traced here: 203 us
  Pallas kernels  63 us (31%)
  waiting for transfers between devices  56.8 us (28%)
  starting transfers between devices  47.5 us (23%)
  other arithmetic  12.1 us (6%)
  blocking collectives  11.1 us (5%)
  local copies, waits for them, and re-layouts  8.55 us (4%)
  between operations  3.56 us (2%)
    all_to_all x3, waiting for transfers between devices, exchange_flat(): lax.all_to_all(x, 'rays', 0, 0, tiled=True, axis_index_groups=flat_groups)  51 us
    pallas_call x1, Pallas kernels, per_device(): pl.pallas_call(fine_kernel, out_shape=corner_shape, grid_spec=pltpu.Prefe...  34 us
    pallas_call x1, Pallas kernels, per_device(): pl.pallas_call(long_kernel, out_shape=corner_shape, grid_spec=pltpu.Prefe...  24 us
    ppermute x6, starting transfers between devices, along_z(): return lax.ppermute(x, 'rays', pairs)  15 us
    all_to_all x3, starting transfers between devices, exchange_flat(): lax.all_to_all(x, 'rays', 0, 0, tiled=True, axis_index_groups=flat_groups)  13.3 us
    all_to_all x1, blocking collectives, per_device(): fine_corners = lax.all_to_all(fine_corners, 'planes', 0, 0, tiled=True)  11.1 us
    all_to_all x1, starting transfers between devices, per_device(): long_corners = lax.all_to_all(long_corners, 'planes', 0, 0, tiled=True)  7.56 us
    all_to_all x1, starting transfers between devices, per_device(): tiles = lax.all_to_all(tile_density, 'planes', 0, 0, tiled=True)  6.5 us
  transfers between devices with their start and end apart: 12, of which 5 were waited for; matrix products, arithmetic and copies ran while one was open for 10% of the time, Pallas kernels for 29%

profile of v1, /device:TPU:1, one launch (start us, length us, event | category | flops | bytes accessed | tf_op | source)
XLA Modules:
  0.0 202.8 jit_solution(15640587697390283164)
XLA Ops:
  0.6 6.5 %all-to-all-start.1 = ((bf16[4,4,32,128]{3,2,1,0:T(8,128)(2,1)}), bf16[4,4,32,128]{3,2,1,0:T(8,128)(2,1)S(1)}, u32[]{:S(2)}, u32[]{:S(2)}) async-start(bf16[4,4,32,128]{3,2,1,0:T(8,128)(2,1)} %param.9), calls=%async_computation.1 | async-start | bytes 262144 | tf_op jit(solution)/shard_map/all_to_all | solution.py:197
  7.1 1.2 dynamic_slice.20
  14.7 2.0 constant_dynamic-slice_fusion
  16.6 2.5 %copy.54 = bf16[1,1,512,2,512]{2,4,3,1,0:T(8,128)(2,1)} copy(bf16[1,1,512,2,512]{4,3,2,1,0:T(2,128)(2,1)S(1)} %constant_dynamic-slice_fusion) | data formatting | bytes 2097152 | tf_op jit(solution)/shard_map/jit(dynamic_index_in_dim)/dynamic_slice | solution.py:220
  19.9 5.1 %all-to-all-start.4 = ((bf16[16,64,512]{2,1,0:T(8,128)(2,1)}), bf16[16,64,512]{2,1,0:T(8,128)(2,1)S(1)}, u32[]{:S(2)}, u32[]{:S(2)}) async-start(bf16[16,64,512]{2,1,0:T(8,128)(2,1)} %bitcast.24), calls=%async_computation.4 | async-start | bytes 2097152 | tf_op jit(solution)/shard_map/all_to_all | solution.py:177
  26.0 16.0 %all-to-all-done.4 = bf16[16,64,512]{2,1,0:T(8,128)(2,1)S(1)} async-done(((bf16[16,64,512]{2,1,0:T(8,128)(2,1)}), bf16[16,64,512]{2,1,0:T(8,128)(2,1)S(1)}, u32[]{:S(2)}, u32[]{:S(2)}) %all-to-all-start.4) | async-done | bytes 1048608 | tf_op jit(solution)/shard_map/all_to_all | solution.py:177
  42.0 5.2 %all-to-all-start = ((bf16[4,4,8320]{2,1,0:T(4,128)(2,1)}), bf16[4,4,8320]{2,1,0:T(4,128)(2,1)S(1)}, u32[]{:S(2)}, u32[]{:S(2)}) async-start(bf16[4,4,8320]{2,1,0:T(4,128)(2,1)} %fusion.1), calls=%async_computation | async-start | bytes 532480 | tf_op jit(solution)/shard_map/all_to_all | solution.py:190
  47.2 6.0 %collective-permute-start.3 = (bf16[64,512]{1,0:T(8,128)(2,1)S(1)}, bf16[64,512]{1,0:T(8,128)(2,1)S(1)}, u32[]{:S(2)}, u32[]{:S(2)}) collective-permute-start(bf16[64,512]{1,0:T(8,128)(2,1)S(1)} %dynamic-slice_bitcast_fusion), channel_id=1, source_target_pairs={{0,192},{4,196},{8,200},{12,204},{16,208},{20,212},{24,216},{28,22... | collective-permute-start | bytes 196616 | tf_op jit(solution)/shard_map/ppermute | solution.py:174
  54.2 2.3 %collective-permute-start.5 = (bf16[64,512]{1,0:T(8,128)(2,1)S(1)}, bf16[64,512]{1,0:T(8,128)(2,1)S(1)}, u32[]{:S(2)}, u32[]{:S(2)}) collective-permute-start(bf16[64,512]{1,0:T(8,128)(2,1)S(1)} %dynamic-slice_bitcast_fusion), channel_id=1, source_target_pairs={{0,64},{4,68},{8,72},{12,76},{16,80},{20,84},{24,88},{28,92},{32,9... | collective-permute-start | bytes 196616 | tf_op jit(solution)/shard_map/ppermute | solution.py:174
  56.8 1.4 collective-permute-start.2
  58.1 4.4 %collective-permute-start.1 = (bf16[4,128,128]{2,1,0:T(8,128)(2,1)S(1)}, bf16[4,128,128]{2,1,0:T(8,128)(2,1)S(1)}, u32[]{:S(2)}, u32[]{:S(2)}) collective-permute-start(bf16[4,128,128]{2,1,0:T(8,128)(2,1)S(1)} %bitcast.56), channel_id=1, source_target_pairs={{0,128},{4,132},{8,136},{12,140},{16,144},{20,148},{24,152},{28,15... | collective-permute-start | bytes 393224 | tf_op jit(solution)/shard_map/ppermute | solution.py:174
  62.6 1.1 broadcast_in_dim.114
  63.7 3.7 %all-to-all-start.5 = ((bf16[16,64,512]{2,1,0:T(8,128)(2,1)}), bf16[16,64,512]{2,1,0:T(8,128)(2,1)S(1)}, u32[]{:S(2)}, u32[]{:S(2)}) async-start(bf16[16,64,512]{2,1,0:T(8,128)(2,1)} %broadcast_in_dim.114), calls=%async_computation.5 | async-start | bytes 2097152 | tf_op jit(solution)/shard_map/all_to_all | solution.py:177
  67.7 3.5 %collective-permute-done.1 = bf16[4,128,128]{2,1,0:T(8,128)(2,1)S(1)} collective-permute-done((bf16[4,128,128]{2,1,0:T(8,128)(2,1)S(1)}, bf16[4,128,128]{2,1,0:T(8,128)(2,1)S(1)}, u32[]{:S(2)}, u32[]{:S(2)}) %collective-permute-start.1) | collective-permute-done | bytes 131104 | tf_op jit(solution)/shard_map/ppermute | solution.py:174
  71.2 2.3 %collective-permute-done = bf16[4,128,128]{2,1,0:T(8,128)(2,1)S(1)} collective-permute-done((bf16[4,128,128]{2,1,0:T(8,128)(2,1)S(1)}, bf16[4,128,128]{2,1,0:T(8,128)(2,1)S(1)}, u32[]{:S(2)}, u32[]{:S(2)}) %collective-permute-start) | collective-permute-done | bytes 131104 | tf_op jit(solution)/shard_map/ppermute | solution.py:174
  73.7 2.5 %select_select_fusion = bf16[16,4,2,128,128]{4,3,2,1,0:T(8,128)(2,1)} fusion(pred[16,4,2]{2,1,0:T(4,128)(4,1)S(1)} %copy.49, pred[16,4,2]{2,1,0:T(4,128)(4,1)S(1)} %copy.48, pred[16,4,2]{2,1,0:T(4,128)(4,1)S(1)} %copy.46, bf16[4,128,128]{2,1,0:T(8,128)(2,1)S(1)} %get-tuple-element.7, bf16[4,128,128]{2,1,0:T(8,128)(2,1)S(1)} %get-tuple-element.8, ...), kind=kLoop, calls=%fused_computation | loop fusion | flops 6291456 | bytes 4718976 | tf_op jit(solution)/shard_map/jit(_where)/select_n | solution.py:210
  76.2 6.6 %all-to-all-done.5 = bf16[16,64,512]{2,1,0:T(8,128)(2,1)S(1)} async-done(((bf16[16,64,512]{2,1,0:T(8,128)(2,1)}), bf16[16,64,512]{2,1,0:T(8,128)(2,1)S(1)}, u32[]{:S(2)}, u32[]{:S(2)}) %all-to-all-start.5) | async-done | bytes 1048608 | tf_op jit(solution)/shard_map/all_to_all | solution.py:177
  82.7 4.5 %all-to-all-start.2 = ((bf16[16,4,2,128,128]{4,3,2,1,0:T(8,128)(2,1)}), bf16[16,4,2,128,128]{4,3,2,1,0:T(8,128)(2,1)}, u32[]{:S(2)}, u32[]{:S(2)}) async-start(bf16[16,4,2,128,128]{4,3,2,1,0:T(8,128)(2,1)} %select_select_fusion), calls=%async_computation.2 | async-start | bytes 8388608 | tf_op jit(solution)/shard_map/all_to_all | solution.py:177
  91.0 24.0 %long_gather.1 = bf16[4,8,8192]{2,1,0:T(8,128)(2,1)} custom-call(s32[2,64]{1,0:T(2,128)S(1)} %reshape.275.start_ref, bf16[2,512,512]{2,1,0:T(8,128)(2,1)S(1)} %bitcast.54, bf16[2,512,512]{2,1,0:T(8,128)(2,1)S(1)} %pad_maximum_fusion.next_ref, f32[4,4,8192]{2,1,0:T(4,128)S(1)} %slice_convert_fusion.cells_ref, bf16[16,128]{1,0:T(8,128)(2,1)S(1)} %fusion.15.select_ref), custom_call_target="tpu_custom_call" | custom-call | tf_op jit(solution)/shard_map/long_gather/pallas_call | solution.py:243
  115.0 28.4 %all-to-all-done.2 = bf16[16,4,2,128,128]{4,3,2,1,0:T(8,128)(2,1)} async-done(((bf16[16,4,2,128,128]{4,3,2,1,0:T(8,128)(2,1)}), bf16[16,4,2,128,128]{4,3,2,1,0:T(8,128)(2,1)}, u32[]{:S(2)}, u32[]{:S(2)}) %all-to-all-start.2) | async-done | bytes 4194336 | tf_op jit(solution)/shard_map/all_to_all | solution.py:177
  143.4 7.6 %all-to-all-start.6 = ((bf16[4,8,8192]{2,1,0:T(8,128)(2,1)}), bf16[4,8,8192]{2,1,0:T(8,128)(2,1)S(1)}, u32[]{:S(2)}, u32[]{:S(2)}) async-start(bf16[4,8,8192]{2,1,0:T(8,128)(2,1)} %long_gather.1), calls=%async_computation.6 | async-start | bytes 1048576 | tf_op jit(solution)/shard_map/all_to_all | solution.py:255
  152.5 34.0 %fine_gather.1 = bf16[4,8,8192]{2,1,0:T(8,128)(2,1)S(1)} custom-call(s32[64]{0:T(128)S(1)} %reshape_squeeze.3.slot_ref, s32[64]{0:T(128)S(1)} %fusion.28.entry_ref, bf16[128,128,128]{2,1,0:T(8,128)(2,1)} %bitcast.17.tiles_ref, f32[4,4,8192]{2,1,0:T(4,128)S(1)} %slice_convert_fusion.cells_ref, bf16[256,128]{1,0:T(8,128)(2,1)S(1)} %copy.52.left_ref, ...), custom_call_target="tpu_custom_call" | custom-call | tf_op jit(solution)/shard_map/fine_gather/pallas_call | solution.py:256
  186.5 11.1 %all_to_all.35.fine_ref = bf16[4,8,8192]{2,1,0:T(8,128)(2,1)} all-to-all(bf16[4,8,8192]{2,1,0:T(8,128)(2,1)S(1)} %fine_gather.1), channel_id=1, replica_groups=mesh['rays'=64,'planes'=4] {'planes'}, dimensions={0} | all-to-all | bytes 1048576 | tf_op jit(solution)/shard_map/all_to_all | solution.py:268
  197.7 5.1 %lens_sum.1 = (f32[4,2,8192]{2,1,0:T(2,128)}, f32[2,8192]{1,0:T(2,128)}) custom-call(bf16[4,8,8192]{2,1,0:T(8,128)(2,1)} %all_to_all.35.fine_ref, bf16[4,8,8192]{2,1,0:T(8,128)(2,1)} %copy-done, f32[4,4,8192]{2,1,0:T(4,128)} %frac_ref.1), custom_call_target="tpu_custom_call" | custom-call | tf_op jit(solution)/shard_map/lens_sum/pallas_call | solution.py:270
  (63 shorter events, 12.4 us)
Async XLA Ops:
  0.6 19.3 %all-to-all-start.1 = ((bf16[4,4,32,128]{3,2,1,0:T(8,128)(2,1)}), bf16[4,4,32,128]{3,2,1,0:T(8,128)(2,1)S(1)}, u32[]{:S(2)}, u32[]{:S(2)}) async-start(bf16[4,4,32,128]{3,2,1,0:T(8,128)(2,1)} %param.9), calls=%async_computation.1 | async-start | bytes 262144 | tf_op jit(solution)/shard_map/all_to_all | solution.py:197
  19.9 22.0 %all-to-all-start.4 = ((bf16[16,64,512]{2,1,0:T(8,128)(2,1)}), bf16[16,64,512]{2,1,0:T(8,128)(2,1)S(1)}, u32[]{:S(2)}, u32[]{:S(2)}) async-start(bf16[16,64,512]{2,1,0:T(8,128)(2,1)} %bitcast.24), calls=%async_computation.4 | async-start | bytes 2097152 | tf_op jit(solution)/shard_map/all_to_all | solution.py:177
  42.0 20.6 %all-to-all-start = ((bf16[4,4,8320]{2,1,0:T(4,128)(2,1)}), bf16[4,4,8320]{2,1,0:T(4,128)(2,1)S(1)}, u32[]{:S(2)}, u32[]{:S(2)}) async-start(bf16[4,4,8320]{2,1,0:T(4,128)(2,1)} %fusion.1), calls=%async_computation | async-start | bytes 532480 | tf_op jit(solution)/shard_map/all_to_all | solution.py:190
  47.2 15.4 %collective-permute-start.3 = (bf16[64,512]{1,0:T(8,128)(2,1)S(1)}, bf16[64,512]{1,0:T(8,128)(2,1)S(1)}, u32[]{:S(2)}, u32[]{:S(2)}) collective-permute-start(bf16[64,512]{1,0:T(8,128)(2,1)S(1)} %dynamic-slice_bitcast_fusion), channel_id=1, source_target_pairs={{0,192},{4,196},{8,200},{12,204},{16,208},{20,212},{24,216},{28,22... | collective-permute-start | bytes 196616 | tf_op jit(solution)/shard_map/ppermute | solution.py:174
  53.2 9.3 %collective-permute-start.4 = (bf16[64,512]{1,0:T(8,128)(2,1)S(1)}, bf16[64,512]{1,0:T(8,128)(2,1)S(1)}, u32[]{:S(2)}, u32[]{:S(2)}) collective-permute-start(bf16[64,512]{1,0:T(8,128)(2,1)S(1)} %dynamic-slice_bitcast_fusion), channel_id=1, source_target_pairs={{0,128},{4,132},{8,136},{12,140},{16,144},{20,148},{24,152},{28,15... | collective-permute-start | bytes 196616 | tf_op jit(solution)/shard_map/ppermute | solution.py:174
  54.2 8.4 %collective-permute-start.5 = (bf16[64,512]{1,0:T(8,128)(2,1)S(1)}, bf16[64,512]{1,0:T(8,128)(2,1)S(1)}, u32[]{:S(2)}, u32[]{:S(2)}) collective-permute-start(bf16[64,512]{1,0:T(8,128)(2,1)S(1)} %dynamic-slice_bitcast_fusion), channel_id=1, source_target_pairs={{0,64},{4,68},{8,72},{12,76},{16,80},{20,84},{24,88},{28,92},{32,9... | collective-permute-start | bytes 196616 | tf_op jit(solution)/shard_map/ppermute | solution.py:174
  56.8 11.0 %collective-permute-start.2 = (bf16[4,128,128]{2,1,0:T(8,128)(2,1)S(1)}, bf16[4,128,128]{2,1,0:T(8,128)(2,1)S(1)}, u32[]{:S(2)}, u32[]{:S(2)}) collective-permute-start(bf16[4,128,128]{2,1,0:T(8,128)(2,1)S(1)} %bitcast.55), channel_id=1, source_target_pairs={{0,192},{4,196},{8,200},{12,204},{16,208},{20,212},{24,216},{28,22... | collective-permute-start | bytes 393224 | tf_op jit(solution)/shard_map/ppermute | solution.py:174
  58.1 13.1 %collective-permute-start.1 = (bf16[4,128,128]{2,1,0:T(8,128)(2,1)S(1)}, bf16[4,128,128]{2,1,0:T(8,128)(2,1)S(1)}, u32[]{:S(2)}, u32[]{:S(2)}) collective-permute-start(bf16[4,128,128]{2,1,0:T(8,128)(2,1)S(1)} %bitcast.56), channel_id=1, source_target_pairs={{0,128},{4,132},{8,136},{12,140},{16,144},{20,148},{24,152},{28,15... | collective-permute-start | bytes 393224 | tf_op jit(solution)/shard_map/ppermute | solution.py:174
  62.5 11.0 %collective-permute-start = (bf16[4,128,128]{2,1,0:T(8,128)(2,1)S(1)}, bf16[4,128,128]{2,1,0:T(8,128)(2,1)S(1)}, u32[]{:S(2)}, u32[]{:S(2)}) collective-permute-start(bf16[4,128,128]{2,1,0:T(8,128)(2,1)S(1)} %bitcast.57), channel_id=1, source_target_pairs={{0,64},{4,68},{8,72},{12,76},{16,80},{20,84},{24,88},{28,92},{32,9... | collective-permute-start | bytes 393224 | tf_op jit(solution)/shard_map/ppermute | solution.py:174
  63.7 19.1 %all-to-all-start.5 = ((bf16[16,64,512]{2,1,0:T(8,128)(2,1)}), bf16[16,64,512]{2,1,0:T(8,128)(2,1)S(1)}, u32[]{:S(2)}, u32[]{:S(2)}) async-start(bf16[16,64,512]{2,1,0:T(8,128)(2,1)} %broadcast_in_dim.114), calls=%async_computation.5 | async-start | bytes 2097152 | tf_op jit(solution)/shard_map/all_to_all | solution.py:177
  82.7 60.7 %all-to-all-start.2 = ((bf16[16,4,2,128,128]{4,3,2,1,0:T(8,128)(2,1)}), bf16[16,4,2,128,128]{4,3,2,1,0:T(8,128)(2,1)}, u32[]{:S(2)}, u32[]{:S(2)}) async-start(bf16[16,4,2,128,128]{4,3,2,1,0:T(8,128)(2,1)} %select_select_fusion), calls=%async_computation.2 | async-start | bytes 8388608 | tf_op jit(solution)/shard_map/all_to_all | solution.py:177
  143.4 43.1 %all-to-all-start.6 = ((bf16[4,8,8192]{2,1,0:T(8,128)(2,1)}), bf16[4,8,8192]{2,1,0:T(8,128)(2,1)S(1)}, u32[]{:S(2)}, u32[]{:S(2)}) async-start(bf16[4,8,8192]{2,1,0:T(8,128)(2,1)} %long_gather.1), calls=%async_computation.6 | async-start | bytes 1048576 | tf_op jit(solution)/shard_map/all_to_all | solution.py:255
  186.5 11.2 %copy-start = (bf16[4,8,8192]{2,1,0:T(8,128)(2,1)}, bf16[4,8,8192]{2,1,0:T(8,128)(2,1)S(1)}, u32[]{:S(2)}) copy-start(bf16[4,8,8192]{2,1,0:T(8,128)(2,1)S(1)} %all-to-all-done.6.long_ref) | copy-start | bytes 1572868

commit v2 on v1

v2 whole, which is shorter than its diff:
```python
import jax
import jax.numpy as jnp
from jax import lax
from jax.experimental import pallas as pl
from jax.experimental.pallas import tpu as pltpu
from jax.sharding import PartitionSpec as P

RATIO = 16
BF = jnp.bfloat16
F32 = jnp.float32
SUB = 16
ZG = 4
TAPS = 6


def kernel_tables(side):
    indices = jnp.arange(side, dtype=jnp.int32)
    offset = (indices[:, None] - indices[None, :]).astype(F32)
    tap_offsets = jnp.arange(-TAPS, TAPS + 1, dtype=jnp.int32).astype(F32)
    tap_total = jnp.sum(jnp.exp(-tap_offsets * tap_offsets / 8.0))
    inside = jnp.abs(offset) <= TAPS
    weight = jnp.where(inside, jnp.exp(-offset * offset / 8.0), 0.0) / tap_total
    smooth_table = weight.astype(BF)
    slope_table = (6.0 * offset * weight / 4.0).astype(BF)
    return (smooth_table, slope_table)


def with_next(table):
    following = jnp.concatenate([table[1:], jnp.zeros_like(table[:1])], axis=0)
    return jnp.concatenate([table.T, following.T], axis=1)


def onehot_tiles(row, tiles, width):
    wide = jnp.broadcast_to(row, (SUB, width)).astype(BF)
    place = lax.broadcasted_iota(jnp.int32, (SUB, width), 0).astype(F32)
    one = jnp.ones((SUB, width), BF)
    zero = jnp.zeros((SUB, width), BF)
    return [
        jnp.where(wide == (place + float(SUB * t)).astype(BF), one, zero) for t in range(tiles)
    ]


def corner_sums(found, columns, select):
    rows = found.shape[0] // 4
    half = found.shape[1] // 2
    results = []
    for h in range(2):
        lanes = slice(h * half, (h + 1) * half)
        column = columns[:, lanes]
        tile_of = [jnp.floor((column + step) * (1.0 / SUB)) for step in (0.0, 1.0)]
        wide = [jnp.broadcast_to(t, (SUB, half)).astype(BF) for t in tile_of]
        kept = [[None, None] for _ in range(4)]
        for t in range(rows // SUB):
            hit = [w == float(t) for w in wide]
            for i in range(4):
                low = found[i * rows + t * SUB : i * rows + (t + 1) * SUB, lanes].astype(BF)
                for s in range(2):
                    kept[i][s] = low if t == 0 else jnp.where(hit[s], low, kept[i][s])
        hot = [onehot_tiles(column + s - SUB * tile_of[s], 1, half)[0] for s in range(2)]
        stacked = jnp.concatenate([kept[i][s] * hot[s] for i in range(4) for s in range(2)], axis=0)
        results.append(jnp.dot(select, stacked, preferred_element_type=F32)[:8])
    return jnp.concatenate(results, axis=1)


def pipelined(count, stages):
    held = {}
    for turn in range(count + len(stages) - 1):
        for s, stage in enumerate(stages):
            item = turn - s
            if 0 <= item < count:
                held[item] = stage(item, held.get(item))


def fine_kernel(whose_ref, slot_ref, entry_ref, tiles_ref, cells_ref, left_ref, slope_ref, smooth_ref, select_ref, out_ref):
    step = pl.program_id(0)
    width = 512
    per_step = out_ref.shape[2] // width
    places, strips = tiles_ref.shape[1:3]
    side = tiles_ref.shape[4]

    def lanes(b):
        return slice(b * width, (b + 1) * width)

    def columns_done(b, _):
        entry = entry_ref[slot_ref[step * per_step + b]]
        source, place = entry // strips, entry % strips
        density = jnp.concatenate([tiles_ref[source, i, place] for i in range(places)], axis=0)
        return lax.dot_general(
            left_ref[...], density, (((1,), (1,)), ((), ())), preferred_element_type=F32
        ).astype(BF)

    def fields(b, partial):
        along_x = jnp.dot(partial[:side], slope_ref[...], preferred_element_type=F32).astype(BF)
        along_y = jnp.dot(partial[side:], smooth_ref[...], preferred_element_type=F32).astype(BF)
        return jnp.concatenate(
            [along_x[:, :side], along_y[:, :side], along_x[:, side:], along_y[:, side:]], axis=0
        )

    def gather_rows(b, table):
        hot = jnp.concatenate(onehot_tiles(cells_ref[0, 0:1, lanes(b)], side // SUB, width), axis=0)
        return jnp.dot(table, hot, preferred_element_type=F32)

    def gather_columns(b, found):
        corners = corner_sums(found, cells_ref[0, 1:2, lanes(b)], select_ref[...])
        out_ref[0, :, lanes(b)] = corners.astype(BF)

    pipelined(per_step, (columns_done, fields, gather_rows, gather_columns))


def long_kernel(whose_ref, start_ref, map_ref, cells_ref, select_ref, out_ref):
    step = pl.program_id(0)
    width = 512
    per_step = out_ref.shape[2] // width
    extent = map_ref.shape[1]
    side = 128
    rows = side + SUB

    def lanes(b):
        return slice(b * width, (b + 1) * width)

    def bases(b):
        row_start = start_ref[0, step * per_step + b]
        col_start = start_ref[1, step * per_step + b]
        row_base = jnp.minimum(row_start // side, extent // side - 2) * side
        col_base = jnp.minimum(col_start // SUB, (extent - rows) // SUB) * SUB
        return row_start, pl.multiple_of(row_base, side), col_start, pl.multiple_of(col_base, SUB)

    def gather_rows(b, _):
        row_start, row_base, _, col_base = bases(b)
        take = (pl.ds(col_base, rows), pl.ds(row_base, 2 * side))
        table = jnp.concatenate([map_ref[(0, *take)], map_ref[(1, *take)]], axis=0)
        table = jnp.concatenate([table, pltpu.roll(table, 2 * side - 1, axis=1)], axis=0)
        row = cells_ref[0, 2:3, lanes(b)] + (row_start - row_base).astype(F32)
        hot = jnp.concatenate(onehot_tiles(row, 2 * side // SUB, width), axis=0)
        return jnp.dot(table, hot, preferred_element_type=F32)

    def gather_columns(b, found):
        _, _, col_start, col_base = bases(b)
        col = cells_ref[0, 3:4, lanes(b)] + (col_start - col_base).astype(F32)
        out_ref[0, :, lanes(b)] = corner_sums(found, col, select_ref[...]).astype(BF)

    pipelined(per_step, (gather_rows, gather_columns))


def table_value(corners, p, q):
    rw0 = (1.0 - p).astype(BF).astype(F32)
    rw1 = p.astype(BF).astype(F32)
    cw0, cw1 = 1.0 - q, q
    v = [corners[i : i + 1] for i in range(8)]
    along_x = (rw0 * v[0] + rw1 * v[4]) * cw0 + (rw0 * v[1] + rw1 * v[5]) * cw1
    along_y = (rw0 * v[2] + rw1 * v[6]) * cw0 + (rw0 * v[3] + rw1 * v[7]) * cw1
    return along_x, along_y


def lens_shift(previous, target):
    shift_x, shift_y = 0.0, 0.0
    for earlier, (x, y) in enumerate(previous):
        factor = (target - earlier) / target
        shift_x, shift_y = shift_x - factor * x, shift_y - factor * y
    return shift_x, shift_y


def final_kernel(fine_ref, long_ref, frac_ref, deflection_ref, source_ref):
    planes = fine_ref.shape[0]
    found = []
    for k in range(planes):
        frac = frac_ref[k]
        sx, sy = lens_shift(found, k)
        fx, fy = table_value(fine_ref[k].astype(F32), frac[0:1] + sx, frac[1:2] + sy)
        lx, ly = table_value(
            long_ref[k].astype(F32), frac[2:3] + sx / RATIO, frac[3:4] + sy / RATIO
        )
        found.append((fx + lx, fy + ly))
        deflection_ref[k, 0:1] = found[k][0]
        deflection_ref[k, 1:2] = found[k][1]
    sx, sy = lens_shift(found, planes)
    source_ref[0:1] = sx
    source_ref[1:2] = sy


def per_device(
    tile_density,
    long_maps,
    map_owner,
    tile_lists,
    block_slots,
    block_windows,
    fine_cells,
    long_cells,
    fractions,
):
    my_row = lax.axis_index("rays")
    plane = lax.axis_index("planes")
    planes, tile_dev, strip, side = tile_density.shape
    extent = long_maps.shape[2]
    list_len = tile_lists.shape[2]
    rays_here = fine_cells.shape[2]
    blocks = block_slots.shape[1]
    ray_count = lax.axis_size("rays")
    level = ray_count // ZG
    my_z, my_xy = my_row // level, my_row % level
    flat_groups = [[z * level + i for i in range(level)] for z in range(ZG)]

    def along_z(x, d):
        pairs = [(r, (r // level + d) % ZG * level + r % level) for r in range(ray_count)]
        return lax.ppermute(x, "rays", pairs)

    def exchange_flat(x):
        return lax.all_to_all(x, "rays", 0, 0, tiled=True, axis_index_groups=flat_groups)

    column = jnp.stack([tile_density] + [along_z(tile_density, d) for d in range(1, ZG)])

    own_map = lax.dynamic_index_in_dim(long_maps[0], plane, 0, keepdims=False)
    own_map = own_map.transpose(1, 2, 0).reshape(level, 2 * extent // level, extent)
    owner = lax.dynamic_index_in_dim(map_owner, plane, 0, keepdims=False)
    pieces = exchange_flat(own_map)
    piece = lax.dynamic_index_in_dim(pieces, owner % level, 0, keepdims=False)

    level_lists = lax.dynamic_slice(tile_lists, (my_z * level, 0, 0), (level, planes, list_len))
    owners = level_lists // tile_dev
    key = jnp.arange(list_len, dtype=jnp.int32) * tile_dev + level_lists % tile_dev
    column_owner = (my_z - jnp.arange(ZG, dtype=jnp.int32)) % ZG * level + my_xy
    mine = owners[:, :, None, :] == column_owner[None, None, :, None]
    first = jnp.min(jnp.where(mine, key[:, :, None, :], tile_dev * list_len), axis=3) % tile_dev
    last = jnp.max(jnp.where(mine, key[:, :, None, :], 0), axis=3) % tile_dev
    wanted = jnp.stack([first, last], axis=3)[..., None, None]
    by_plane = column.transpose(1, 0, 2, 3, 4)
    outgoing = jnp.broadcast_to(
        by_plane[None, :, :, None, 0], (level, planes, ZG, 2, strip, side)
    )
    for t in range(1, tile_dev):
        outgoing = jnp.where(wanted == t, by_plane[None, :, :, None, t], outgoing)
    outgoing, piece = lax.optimization_barrier((outgoing, piece))
    incoming = lax.all_to_all(
        outgoing.reshape(level * planes, ZG * 2, strip, side),
        ("rays", "planes"),
        0,
        0,
        tiled=True,
        axis_index_groups=[
            list(range(z * level * planes, (z + 1) * level * planes)) for z in range(ZG)
        ],
    ).reshape(level, planes, ZG * 2, strip, side)

    distance = (my_z - owner // level) % ZG
    chosen = piece
    for d in range(1, ZG):
        chosen = jnp.where(distance == d, along_z(piece, d), chosen)

    my_list = lax.dynamic_slice(tile_lists, (my_row, plane, 0), (1, 1, list_len))[0, 0]
    my_owner = my_list // tile_dev
    place = jnp.arange(list_len, dtype=jnp.int32)
    repeat = (my_owner[:, None] == my_owner[None, :]) & (place[:, None] > place[None, :])
    rank = jnp.max(repeat.astype(jnp.int32), axis=1)
    entry = my_owner % level * (2 * ZG) + (my_z - my_owner // level) % ZG * 2 + rank

    block_slots, block_windows, fine_cells, long_cells, _ = lax.optimization_barrier(
        (block_slots, block_windows, fine_cells, long_cells, column[ZG - 1, 0, 0, 0, :1])
    )
    small = jnp.concatenate(
        [block_slots[:, None, :], block_windows // SUB, block_windows % SUB], axis=1
    ).reshape(planes, 1, 5 * blocks)
    small = jnp.pad(small, ((0, 0), (0, 3), (0, 128 - 5 * blocks)))
    cells = jnp.concatenate([fine_cells, long_cells], axis=1)
    ray_info = jnp.concatenate([cells, small], axis=2).astype(BF)
    arrived = [lax.dynamic_index_in_dim(ray_info, plane, 0, keepdims=False)]
    for d in range(1, planes):
        pairs = [(i, (i + d) % planes) for i in range(planes)]
        sent = lax.dynamic_index_in_dim(ray_info, (plane + d) % planes, 0, keepdims=False)
        arrived.append(lax.ppermute(sent, "planes", pairs))
    arrived = jnp.stack(arrived)
    cells = arrived[:, :, :rays_here].astype(F32)
    small = arrived[:, 0, rays_here : rays_here + 5 * blocks].astype(jnp.int32)
    small = small.reshape(planes, 5, blocks)
    turn = (plane - jnp.arange(planes)) % planes
    small = jnp.sum(
        jnp.where(turn[:, None] == jnp.arange(planes), 1, 0)[:, :, None, None] * small[None], axis=1
    )
    slots = small[:, 0].reshape(planes * blocks)
    starts = (small[:, 1:3] * SUB + small[:, 3:5]).transpose(1, 0, 2).reshape(2, planes * blocks)
    whose = plane.reshape(1)

    chosen, incoming = lax.optimization_barrier((chosen, incoming))
    whole = exchange_flat(jnp.broadcast_to(chosen[None], (level, *chosen.shape)))
    whole = whole.reshape(2, extent, extent)

    select = (jnp.arange(8 * SUB)[None, :] // SUB == jnp.arange(SUB)[:, None]).astype(BF)
    smooth_table, slope_table = kernel_tables(side)
    left = jnp.concatenate([smooth_table, slope_table], axis=0)
    wide = 4096
    per_plane = rays_here // wide
    vmem = pl.BlockSpec(memory_space=pltpu.VMEM)
    cell_spec = pl.BlockSpec(
        (1, 4, wide),
        lambda g, whose, *_: ((whose[0] + planes - g // per_plane) % planes, 0, g % per_plane),
    )
    out_spec = pl.BlockSpec((1, 8, wide), lambda g, *_: (g // per_plane, 0, g % per_plane))
    corner_shape = jax.ShapeDtypeStruct((planes, 8, rays_here), BF)
    params = pltpu.CompilerParams(vmem_limit_bytes=48 << 20)
    fine_corners = pl.pallas_call(
        fine_kernel,
        out_shape=corner_shape,
        grid_spec=pltpu.PrefetchScalarGridSpec(
            num_scalar_prefetch=3,
            grid=(planes * per_plane,),
            in_specs=[vmem, cell_spec, vmem, vmem, vmem, vmem],
            out_specs=out_spec,
        ),
        compiler_params=params,
        name="fine_gather",
    )(whose, slots, entry, incoming, cells, left, with_next(slope_table), with_next(smooth_table), select)
    fine_corners, whole = lax.optimization_barrier((fine_corners, whole))
    fine_corners = lax.all_to_all(fine_corners, "planes", 0, 0, tiled=True)
    long_corners = pl.pallas_call(
        long_kernel,
        out_shape=corner_shape,
        grid_spec=pltpu.PrefetchScalarGridSpec(
            num_scalar_prefetch=2,
            grid=(planes * per_plane,),
            in_specs=[vmem, cell_spec, vmem],
            out_specs=out_spec,
        ),
        compiler_params=params,
        name="long_gather",
    )(whose, starts, whole, cells, select)
    long_corners, fine_corners = lax.optimization_barrier((long_corners, fine_corners))
    long_corners = lax.all_to_all(long_corners, "planes", 0, 0, tiled=True)
    wide = 2048

    return pl.pallas_call(
        final_kernel,
        out_shape=(
            jax.ShapeDtypeStruct((planes, 2, rays_here), F32),
            jax.ShapeDtypeStruct((2, rays_here), F32),
        ),
        grid=(rays_here // wide,),
        in_specs=[
            pl.BlockSpec((planes, 8, wide), lambda g: (0, 0, g)),
            pl.BlockSpec((planes, 8, wide), lambda g: (0, 0, g)),
            pl.BlockSpec((planes, 4, wide), lambda g: (0, 0, g)),
        ],
        out_specs=(
            pl.BlockSpec((planes, 2, wide), lambda g: (0, 0, g)),
            pl.BlockSpec((2, wide), lambda g: (0, g)),
        ),
        name="lens_sum",
    )(fine_corners, long_corners, fractions)


def solution(mesh):
    return jax.shard_map(
        per_device,
        mesh=mesh,
        in_specs=(
            P(None, "rays", "planes", None),
            P("rays", None, None, None, None),
            P(),
            P(),
            P(None, ("rays", "planes")),
            P(None, None, ("rays", "planes")),
            P(None, None, ("rays", "planes")),
            P(None, None, ("rays", "planes")),
            P(None, None, ("rays", "planes")),
        ),
        out_specs=(P(None, None, ("rays", "planes")), P(None, ("rays", "planes"))),
        check_vma=False,
    )
```

time: 204 us -> 177 us (0.87)
  Pallas kernels: 63 us -> 41.1 us
  other arithmetic: 12.1 us -> 8.74 us
  starting transfers between devices: 47.5 us -> 44.9 us
    ppermute x0 -> x3, waiting for transfers between devices: none -> 45.1 us  [per_device(): arrived.append(lax.ppermute(sent, 'planes', pairs))]
    all_to_all x3 -> x2, waiting for transfers between devices: 51 us -> 6.26 us  [exchange_flat(): lax.all_to_all(x, 'rays', 0, 0, tiled=True, axis_index_groups=flat_groups)]
    pallas_call x1, Pallas kernels: 34 us -> 19.9 us  [per_device(): pl.pallas_call(fine_kernel, out_shape=corner_shape, grid_spec=pltpu.Prefe...]
    pallas_call x1, Pallas kernels: 24 us -> 16.1 us  [per_device(): pl.pallas_call(long_kernel, out_shape=corner_shape, grid_spec=pltpu.Prefe...]
    all_to_all x3 -> x2, starting transfers between devices: 19.2 us -> 12.4 us  [the longest x1 8.25 us: per_device(): lax.all_to_all(outgoing.reshape(level * planes, ZG * 2, strip, side), ('r...]
    another operation x4 -> x3, other arithmetic: 2.87 us -> 0.21 us
    select_n x2 -> x5, other arithmetic: 2.51 us -> 4.81 us  [the longest x1 4.7 us: per_device(): outgoing = jnp.where(wanted == t, by_plane[None, :, :, None, t], outgoing)]
    ppermute x0 -> x3, starting transfers between devices: none -> 2.23 us  [per_device(): arrived.append(lax.ppermute(sent, 'planes', pairs))]
  transfers between devices with their start and end apart: 12 -> 13, of which waited for: 5 -> 7; matrix products, arithmetic and copies ran while one was open for 10% -> 9% of each run, Pallas kernels for 29% -> 20%
where the time goes in v2:
time: 177 us; the launch traced here: 176 us
  waiting for transfers between devices  58.8 us (33%)
  starting transfers between devices  44.9 us (25%)
  Pallas kernels  41.1 us (23%)
  blocking collectives  11 us (6%)
  other arithmetic  8.74 us (5%)
  local copies, waits for them, and re-layouts  7.76 us (4%)
  between operations  3.82 us (2%)
    ppermute x3, waiting for transfers between devices, per_device(): arrived.append(lax.ppermute(sent, 'planes', pairs))  45.1 us
    pallas_call x1, Pallas kernels, per_device(): pl.pallas_call(fine_kernel, out_shape=corner_shape, grid_spec=pltpu.Prefe...  19.9 us
    pallas_call x1, Pallas kernels, per_device(): pl.pallas_call(long_kernel, out_shape=corner_shape, grid_spec=pltpu.Prefe...  16.1 us
    all_to_all x2, starting transfers between devices, exchange_flat(): lax.all_to_all(x, 'rays', 0, 0, tiled=True, axis_index_groups=flat_groups)  15.4 us
    ppermute x6, starting transfers between devices, along_z(): return lax.ppermute(x, 'rays', pairs)  14.9 us
    all_to_all x1, blocking collectives, per_device(): long_corners = lax.all_to_all(long_corners, 'planes', 0, 0, tiled=True)  11 us
    all_to_all x1, starting transfers between devices, per_device(): lax.all_to_all(outgoing.reshape(level * planes, ZG * 2, strip, side), ('r...  8.25 us
    ppermute x6, waiting for transfers between devices, along_z(): return lax.ppermute(x, 'rays', pairs)  7.4 us
  transfers between devices with their start and end apart: 13, of which 7 were waited for; matrix products, arithmetic and copies ran while one was open for 9% of the time, Pallas kernels for 20%

profile of v2, /device:TPU:1, one launch (start us, length us, event | category | flops | bytes accessed | tf_op | source)
XLA Modules:
  0.0 176.1 jit_solution(15906288226713506660)
XLA Ops:
  0.7 3.9 %collective-permute-start.3 = (bf16[4,4,32,128]{3,2,1,0:T(8,128)(2,1)}, bf16[4,4,32,128]{3,2,1,0:T(8,128)(2,1)S(1)}, u32[]{:S(2)}, u32[]{:S(2)}) collective-permute-start(bf16[4,4,32,128]{3,2,1,0:T(8,128)(2,1)} %param.9), channel_id=1, source_target_pairs={{0,64},{4,68},{8,72},{12,76},{16,80},{20,84},{24,88},{28,92},{32,9... | collective-permute-start | bytes 393224 | tf_op jit(solution)/shard_map/ppermute | solution.py:206
  4.5 5.1 %collective-permute-start.4 = (bf16[4,4,32,128]{3,2,1,0:T(8,128)(2,1)}, bf16[4,4,32,128]{3,2,1,0:T(8,128)(2,1)S(1)}, u32[]{:S(2)}, u32[]{:S(2)}) collective-permute-start(bf16[4,4,32,128]{3,2,1,0:T(8,128)(2,1)} %param.9), channel_id=1, source_target_pairs={{0,128},{4,132},{8,136},{12,140},{16,144},{20,148},{24,152},{28,15... | collective-permute-start | bytes 393224 | tf_op jit(solution)/shard_map/ppermute | solution.py:206
  9.7 2.4 %collective-permute-start.5 = (bf16[4,4,32,128]{3,2,1,0:T(8,128)(2,1)}, bf16[4,4,32,128]{3,2,1,0:T(8,128)(2,1)S(1)}, u32[]{:S(2)}, u32[]{:S(2)}) collective-permute-start(bf16[4,4,32,128]{3,2,1,0:T(8,128)(2,1)} %param.9), channel_id=1, source_target_pairs={{0,192},{4,196},{8,200},{12,204},{16,208},{20,212},{24,216},{28,22... | collective-permute-start | bytes 393224 | tf_op jit(solution)/shard_map/ppermute | solution.py:206
  12.0 1.9 %constant_dynamic-slice_fusion = bf16[1,1,512,2,512]{4,3,2,1,0:T(2,128)(2,1)S(1)} fusion(bf16[1,4,512,2,512]{4,3,2,1,0:T(2,128)(2,1)} %param.10, s32[]{:T(128)S(6)} %select_n.229), kind=kLoop, calls=%fused_computation.95 | loop fusion | bytes 2097156 | tf_op jit(solution)/shard_map/jit(dynamic_index_in_dim)/dynamic_slice | solution.py:213
  14.0 2.5 %copy.48 = bf16[1,1,512,2,512]{2,4,3,1,0:T(8,128)(2,1)} copy(bf16[1,1,512,2,512]{4,3,2,1,0:T(2,128)(2,1)S(1)} %constant_dynamic-slice_fusion) | data formatting | bytes 2097152 | tf_op jit(solution)/shard_map/jit(dynamic_index_in_dim)/dynamic_slice | solution.py:213
  16.5 6.8 %all-to-all-start = ((bf16[16,64,512]{2,1,0:T(8,128)(2,1)}), bf16[16,64,512]{2,1,0:T(8,128)(2,1)S(1)}, u32[]{:S(2)}, u32[]{:S(2)}) async-start(bf16[16,64,512]{2,1,0:T(8,128)(2,1)} %bitcast.24), calls=%async_computation | async-start | bytes 2097152 | tf_op jit(solution)/shard_map/all_to_all | solution.py:209
  27.5 4.7 %select_select_fusion = bf16[16,4,4,2,32,128]{5,4,3,2,1,0:T(8,128)(2,1)} fusion(pred[16,4,4,2]{3,2,1,0:T(4,128)(4,1)S(1)} %copy.45, pred[16,4,4,2]{3,2,1,0:T(4,128)(4,1)S(1)} %copy.43, pred[16,4,4,2]{3,2,1,0:T(4,128)(4,1)S(1)} %copy.41, bf16[4,4,32,128]{3,2,0,1:T(8,128)(2,1)S(1)} %get-tuple-element.30, bf16[4,4,32,128]{3,2,0,1:T(8,128)(2,1)S(1)} %get-tuple-element.33, ...), kind=kLoop, calls=%fused_computation | loop fusion | flops 6291456 | bytes 4720128 | tf_op jit(solution)/shard_map/jit(_where)/select_n | solution.py:232
  32.2 6.3 %all-to-all-done = bf16[16,64,512]{2,1,0:T(8,128)(2,1)S(1)} async-done(((bf16[16,64,512]{2,1,0:T(8,128)(2,1)}), bf16[16,64,512]{2,1,0:T(8,128)(2,1)S(1)}, u32[]{:S(2)}, u32[]{:S(2)}) %all-to-all-start) | async-done | bytes 1048608 | tf_op jit(solution)/shard_map/all_to_all | solution.py:209
  38.5 8.2 %all-to-all-start.1 = ((bf16[64,8,32,128]{3,2,1,0:T(8,128)(2,1)}), bf16[64,8,32,128]{3,2,1,0:T(8,128)(2,1)}, u32[]{:S(2)}, u32[]{:S(2)}) async-start(bf16[64,8,32,128]{3,2,1,0:T(8,128)(2,1)} %bitcast.58), calls=%async_computation.1 | async-start | bytes 8388608 | tf_op jit(solution)/shard_map/all_to_all | solution.py:234
  47.6 1.7 collective-permute-start
  53.5 42.6 %collective-permute-done = bf16[4,8320]{1,0:T(4,128)(2,1)S(1)} collective-permute-done((bf16[4,8320]{1,0:T(4,128)(2,1)S(1)}, bf16[4,8320]{1,0:T(4,128)(2,1)S(1)}, u32[]{:S(2)}, u32[]{:S(2)}) %collective-permute-start) | collective-permute-done | bytes 66592 | tf_op jit(solution)/shard_map/ppermute | solution.py:270
  96.1 1.6 collective-permute-done.1
  97.7 1.0 collective-permute-done.2
  98.9 3.1 %collective-permute-start.7 = (bf16[64,512]{1,0:T(8,128)(2,1)S(1)}, bf16[64,512]{1,0:T(8,128)(2,1)S(1)}, u32[]{:S(2)}, u32[]{:S(2)}) collective-permute-start(bf16[64,512]{1,0:T(8,128)(2,1)S(1)} %dynamic-slice_bitcast_fusion.3), channel_id=1, source_target_pairs={{0,128},{4,132},{8,136},{12,140},{16,144},{20,148},{24,152},{28,15... | collective-permute-start | bytes 196616 | tf_op jit(solution)/shard_map/ppermute | solution.py:206
  102.4 1.1 collective-permute-done.6
  103.5 2.8 %collective-permute-done.7 = bf16[64,512]{1,0:T(8,128)(2,1)S(1)} collective-permute-done((bf16[64,512]{1,0:T(8,128)(2,1)S(1)}, bf16[64,512]{1,0:T(8,128)(2,1)S(1)}, u32[]{:S(2)}, u32[]{:S(2)}) %collective-permute-start.7) | collective-permute-done | bytes 65568 | tf_op jit(solution)/shard_map/ppermute | solution.py:206
  106.3 3.5 %collective-permute-done.8 = bf16[64,512]{1,0:T(8,128)(2,1)S(1)} collective-permute-done((bf16[64,512]{1,0:T(8,128)(2,1)S(1)}, bf16[64,512]{1,0:T(8,128)(2,1)S(1)}, u32[]{:S(2)}, u32[]{:S(2)}) %collective-permute-start.8) | collective-permute-done | bytes 65568 | tf_op jit(solution)/shard_map/ppermute | solution.py:206
  109.8 1.1 broadcast_in_dim.124
  110.9 8.6 %all-to-all-start.2 = ((bf16[16,64,512]{2,1,0:T(8,128)(2,1)}), bf16[16,64,512]{2,1,0:T(8,128)(2,1)S(1)}, u32[]{:S(2)}, u32[]{:S(2)}) async-start(bf16[16,64,512]{2,1,0:T(8,128)(2,1)} %broadcast_in_dim.124), calls=%async_computation.2 | async-start | bytes 2097152 | tf_op jit(solution)/shard_map/all_to_all | solution.py:209
  119.7 19.9 %fine_gather.1 = bf16[4,8,8192]{2,1,0:T(8,128)(2,1)} custom-call(s32[1]{0:T(128)} %bitcast.whose_ref, s32[64]{0:T(128)S(1)} %reshape_squeeze.3.slot_ref, s32[64]{0:T(128)S(1)} %fusion.30.entry_ref, bf16[16,4,8,32,128]{4,3,2,1,0:T(8,128)(2,1)} %bitcast.27.tiles_ref, f32[4,4,8192]{2,1,0:T(4,128)S(1)} %fusion.2.cells_ref, bf16[256,128]{1,0:T(8,128)(2,1)S(1)} %copy.51.left_ref, ...), custom_call_target="tpu_custom_call" | custom-call | tf_op jit(solution)/shard_map/fine_gather/pallas_call | solution.py:300
  139.6 4.2 %all-to-all-start.3 = ((bf16[4,8,8192]{2,1,0:T(8,128)(2,1)}), bf16[4,8,8192]{2,1,0:T(8,128)(2,1)S(1)}, u32[]{:S(2)}, u32[]{:S(2)}) async-start(bf16[4,8,8192]{2,1,0:T(8,128)(2,1)} %fine_gather.1), calls=%async_computation.3 | async-start | bytes 1048576 | tf_op jit(solution)/shard_map/all_to_all | solution.py:313
  143.9 16.1 %long_gather.1 = bf16[4,8,8192]{2,1,0:T(8,128)(2,1)S(1)} custom-call(s32[1]{0:T(128)} %bitcast.whose_ref, s32[2,64]{1,0:T(2,128)S(1)} %reshape.312.start_ref, bf16[2,512,512]{2,1,0:T(8,128)(2,1)S(1)} %bitcast.57, f32[4,4,8192]{2,1,0:T(4,128)S(1)} %fusion.2.cells_ref, bf16[16,128]{1,0:T(8,128)(2,1)S(1)} %fusion.19.select_ref), custom_call_target="tpu_custom_call" | custom-call | tf_op jit(solution)/shard_map/long_gather/pallas_call | solution.py:314
  160.0 11.0 %all_to_all.25.long_ref = bf16[4,8,8192]{2,1,0:T(8,128)(2,1)} all-to-all(bf16[4,8,8192]{2,1,0:T(8,128)(2,1)S(1)} %long_gather.1), channel_id=1, replica_groups=mesh['rays'=64,'planes'=4] {'planes'}, dimensions={0} | all-to-all | bytes 1048576 | tf_op jit(solution)/shard_map/all_to_all | solution.py:327
  171.0 5.1 %lens_sum.1 = (f32[4,2,8192]{2,1,0:T(2,128)}, f32[2,8192]{1,0:T(2,128)}) custom-call(bf16[4,8,8192]{2,1,0:T(8,128)(2,1)} %copy-done, bf16[4,8,8192]{2,1,0:T(8,128)(2,1)} %all_to_all.25.long_ref, f32[4,4,8192]{2,1,0:T(4,128)} %frac_ref.1), custom_call_target="tpu_custom_call" | custom-call | tf_op jit(solution)/shard_map/lens_sum/pallas_call | solution.py:330
  (82 shorter events, 7.3 us)
Async XLA Ops:
  0.6 26.8 %copy-start.3 = (bf16[4,4,32,128]{3,2,1,0:T(8,128)(2,1)S(1)}, bf16[4,4,32,128]{3,2,1,0:T(8,128)(2,1)}, u32[]{:S(2)}) copy-start(bf16[4,4,32,128]{3,2,1,0:T(8,128)(2,1)} %param.9) | copy-start | bytes 393220
  0.6 22.6 %copy-start.4 = (s32[64,4,64]{2,1,0:T(4,128)S(1)}, s32[64,4,64]{2,1,0:T(4,128)}, u32[]{:S(2)}) copy-start(s32[64,4,64]{2,1,0:T(4,128)} %param.12) | copy-start | bytes 196612
  0.7 23.5 %copy-start.7 = (s32[4]{0:T(128)S(1)}, s32[4]{0:T(128)}, u32[]{:S(2)}) copy-start(s32[4]{0:T(128)} %param.11) | copy-start | bytes 52
  0.7 26.7 %collective-permute-start.3 = (bf16[4,4,32,128]{3,2,1,0:T(8,128)(2,1)}, bf16[4,4,32,128]{3,2,1,0:T(8,128)(2,1)S(1)}, u32[]{:S(2)}, u32[]{:S(2)}) collective-permute-start(bf16[4,4,32,128]{3,2,1,0:T(8,128)(2,1)} %param.9), channel_id=1, source_target_pairs={{0,64},{4,68},{8,72},{12,76},{16,80},{20,84},{24,88},{28,92},{32,9... | collective-permute-start | bytes 393224 | tf_op jit(solution)/shard_map/ppermute | solution.py:206
  4.5 22.8 %collective-permute-start.4 = (bf16[4,4,32,128]{3,2,1,0:T(8,128)(2,1)}, bf16[4,4,32,128]{3,2,1,0:T(8,128)(2,1)S(1)}, u32[]{:S(2)}, u32[]{:S(2)}) collective-permute-start(bf16[4,4,32,128]{3,2,1,0:T(8,128)(2,1)} %param.9), channel_id=1, source_target_pairs={{0,128},{4,132},{8,136},{12,140},{16,144},{20,148},{24,152},{28,15... | collective-permute-start | bytes 393224 | tf_op jit(solution)/shard_map/ppermute | solution.py:206
  9.7 17.7 %collective-permute-start.5 = (bf16[4,4,32,128]{3,2,1,0:T(8,128)(2,1)}, bf16[4,4,32,128]{3,2,1,0:T(8,128)(2,1)S(1)}, u32[]{:S(2)}, u32[]{:S(2)}) collective-permute-start(bf16[4,4,32,128]{3,2,1,0:T(8,128)(2,1)} %param.9), channel_id=1, source_target_pairs={{0,192},{4,196},{8,200},{12,204},{16,208},{20,212},{24,216},{28,22... | collective-permute-start | bytes 393224 | tf_op jit(solution)/shard_map/ppermute | solution.py:206
  16.5 22.0 %all-to-all-start = ((bf16[16,64,512]{2,1,0:T(8,128)(2,1)}), bf16[16,64,512]{2,1,0:T(8,128)(2,1)S(1)}, u32[]{:S(2)}, u32[]{:S(2)}) async-start(bf16[16,64,512]{2,1,0:T(8,128)(2,1)} %bitcast.24), calls=%async_computation | async-start | bytes 2097152 | tf_op jit(solution)/shard_map/all_to_all | solution.py:209
  38.5 8.3 %copy-start.6 = (s32[4,16]{1,0:T(4,128)S(1)}, s32[4,16]{1,0:T(4,128)}, u32[]{:S(2)}) copy-start(s32[4,16]{1,0:T(4,128)} %param.13) | copy-start | bytes 772
  38.5 8.4 %copy-start.5 = (s32[4,2,16]{2,1,0:T(2,128)S(1)}, s32[4,2,16]{2,1,0:T(2,128)}, u32[]{:S(2)}) copy-start(s32[4,2,16]{2,1,0:T(2,128)} %param.14) | copy-start | bytes 1540
  38.5 8.5 %copy-start.1 = (s32[4,2,8192]{2,1,0:T(2,128)S(1)}, s32[4,2,8192]{2,1,0:T(2,128)}, u32[]{:S(2)}) copy-start(s32[4,2,8192]{2,1,0:T(2,128)} %param.15) | copy-start | bytes 786436
  38.5 8.6 %copy-start.2 = (s32[4,2,8192]{2,1,0:T(2,128)S(1)}, s32[4,2,8192]{2,1,0:T(2,128)}, u32[]{:S(2)}) copy-start(s32[4,2,8192]{2,1,0:T(2,128)} %param.16) | copy-start | bytes 786436
  38.5 71.3 %all-to-all-start.1 = ((bf16[64,8,32,128]{3,2,1,0:T(8,128)(2,1)}), bf16[64,8,32,128]{3,2,1,0:T(8,128)(2,1)}, u32[]{:S(2)}, u32[]{:S(2)}) async-start(bf16[64,8,32,128]{3,2,1,0:T(8,128)(2,1)} %bitcast.58), calls=%async_computation.1 | async-start | bytes 8388608 | tf_op jit(solution)/shard_map/all_to_all | solution.py:234
  47.6 48.4 %collective-permute-start = (bf16[4,8320]{1,0:T(4,128)(2,1)S(1)}, bf16[4,8320]{1,0:T(4,128)(2,1)S(1)}, u32[]{:S(2)}, u32[]{:S(2)}) collective-permute-start(bf16[4,8320]{1,0:T(4,128)(2,1)S(1)} %get-tuple-element.37), channel_id=1, source_target_pairs={{0,1},{1,2},{2,3},{3,0},{4,5},{5,6},{6,7},{7,4},{8,9},{9,10},{10,1... | collective-permute-start | bytes 199688 | tf_op jit(solution)/shard_map/ppermute | solution.py:270
  49.4 48.3 %collective-permute-start.1 = (bf16[4,8320]{1,0:T(4,128)(2,1)S(1)}, bf16[4,8320]{1,0:T(4,128)(2,1)S(1)}, u32[]{:S(2)}, u32[]{:S(2)}) collective-permute-start(bf16[4,8320]{1,0:T(4,128)(2,1)S(1)} %get-tuple-element.36), channel_id=1, source_target_pairs={{0,2},{1,3},{2,0},{3,1},{4,6},{5,7},{6,4},{7,5},{8,10},{9,11},{10,... | collective-permute-start | bytes 199688 | tf_op jit(solution)/shard_map/ppermute | solution.py:270
  49.7 48.9 %collective-permute-start.2 = (bf16[4,8320]{1,0:T(4,128)(2,1)S(1)}, bf16[4,8320]{1,0:T(4,128)(2,1)S(1)}, u32[]{:S(2)}, u32[]{:S(2)}) collective-permute-start(bf16[4,8320]{1,0:T(4,128)(2,1)S(1)} %get-tuple-element.35), channel_id=1, source_target_pairs={{0,3},{1,0},{2,1},{3,2},{4,7},{5,4},{6,5},{7,6},{8,11},{9,8},{10,9... | collective-permute-start | bytes 199688 | tf_op jit(solution)/shard_map/ppermute | solution.py:270
  98.7 4.7 %collective-permute-start.6 = (bf16[64,512]{1,0:T(8,128)(2,1)S(1)}, bf16[64,512]{1,0:T(8,128)(2,1)S(1)}, u32[]{:S(2)}, u32[]{:S(2)}) collective-permute-start(bf16[64,512]{1,0:T(8,128)(2,1)S(1)} %dynamic-slice_bitcast_fusion.3), channel_id=1, source_target_pairs={{0,192},{4,196},{8,200},{12,204},{16,208},{20,212},{24,216},{28,22... | collective-permute-start | bytes 196616 | tf_op jit(solution)/shard_map/ppermute | solution.py:206
  98.9 7.4 %collective-permute-start.7 = (bf16[64,512]{1,0:T(8,128)(2,1)S(1)}, bf16[64,512]{1,0:T(8,128)(2,1)S(1)}, u32[]{:S(2)}, u32[]{:S(2)}) collective-permute-start(bf16[64,512]{1,0:T(8,128)(2,1)S(1)} %dynamic-slice_bitcast_fusion.3), channel_id=1, source_target_pairs={{0,128},{4,132},{8,136},{12,140},{16,144},{20,148},{24,152},{28,15... | collective-permute-start | bytes 196616 | tf_op jit(solution)/shard_map/ppermute | solution.py:206
  102.0 7.7 %collective-permute-start.8 = (bf16[64,512]{1,0:T(8,128)(2,1)S(1)}, bf16[64,512]{1,0:T(8,128)(2,1)S(1)}, u32[]{:S(2)}, u32[]{:S(2)}) collective-permute-start(bf16[64,512]{1,0:T(8,128)(2,1)S(1)} %dynamic-slice_bitcast_fusion.3), channel_id=1, source_target_pairs={{0,64},{4,68},{8,72},{12,76},{16,80},{20,84},{24,88},{28,92},{32,9... | collective-permute-start | bytes 196616 | tf_op jit(solution)/shard_map/ppermute | solution.py:206
  110.9 28.8 %all-to-all-start.2 = ((bf16[16,64,512]{2,1,0:T(8,128)(2,1)}), bf16[16,64,512]{2,1,0:T(8,128)(2,1)S(1)}, u32[]{:S(2)}, u32[]{:S(2)}) async-start(bf16[16,64,512]{2,1,0:T(8,128)(2,1)} %broadcast_in_dim.124), calls=%async_computation.2 | async-start | bytes 2097152 | tf_op jit(solution)/shard_map/all_to_all | solution.py:209
  139.6 20.4 %all-to-all-start.3 = ((bf16[4,8,8192]{2,1,0:T(8,128)(2,1)}), bf16[4,8,8192]{2,1,0:T(8,128)(2,1)S(1)}, u32[]{:S(2)}, u32[]{:S(2)}) async-start(bf16[4,8,8192]{2,1,0:T(8,128)(2,1)} %fine_gather.1), calls=%async_computation.3 | async-start | bytes 1048576 | tf_op jit(solution)/shard_map/all_to_all | solution.py:313
  160.0 11.0 %copy-start = (bf16[4,8,8192]{2,1,0:T(8,128)(2,1)}, bf16[4,8,8192]{2,1,0:T(8,128)(2,1)S(1)}, u32[]{:S(2)}) copy-start(bf16[4,8,8192]{2,1,0:T(8,128)(2,1)S(1)} %all-to-all-done.3.fine_ref) | copy-start | bytes 1572868
